TPU v7x, 32 devices: a whole 2x2x4 slice. The times are simulated.
32 devices in a mesh: gx: 8 (over z, x), gy: 4 (over y, core).
Axes of the slice: x: 2, y: 2, z: 4, core: 2. Of those that a mesh axis runs over, the one named last changes fastest.
Arguments:
- positions: float32 [3, 65536], P(None, ('gx', 'gy')), may hold values from -6 to 6
- velocities: float32 [3, 65536], P(None, ('gx', 'gy')), may hold values from -6 to 6
- masses: float32 [65536], P(('gx', 'gy')), may hold values from 0.25 to 4
- labels: int32 [65536, 1], P(('gx', 'gy')), may hold values from 0 to 255; in each aligned block of 2048 rows (0 to 2047, 2048 to 4095, ...) at most 16 rows name the same one
- owner_slot: int32 [256], replicated, may hold values from 0 to 255, each once
- group_cap: int32 [256], replicated, may hold values from 512 to 4095
Outputs:
- compact_index: int32 [65536], P(('gx', 'gy'))
- potential: float32 [65536], P(('gx', 'gy'))
- binding: float32 [65536], P(('gx', 'gy'))
- catalog: float32 [4, 256], P(None, ('gx', 'gy'))
Inputs may be any that keep to these rules, and one draw needn't show every extreme that they name: `labels`: on each device's 2048 particles no label occurs more than 16 times; some label occurs exactly 16 times in some devices' particles; every label occurs somewhere. `owner_slot` is a permutation. Group g is owned by device owner_slot[g] // 8 (devices numbered along gx then gy) as its local group owner_slot[g] % 8.
All inputs are finite; a program needn't handle non-finite values.
Results may differ from a plain program's by a relative error of at most 0.0003.
Values sent between devices are 32-bit elements; how exact they have to be, the bound alone decides.
No kernel may reach another device: no remote copies, remote signals or barrier semaphores. Data moves between devices by JAX's collectives and lax.ppermute only.
A program may use at most 64 MiB of HBM per device.

v0:
```python
import jax
import jax.numpy as jnp
from jax import lax
from jax.sharding import PartitionSpec as P

CAP = 2048


softening_sq = 0.0025


def potential_of(group_block, live_count):
    coords = group_block[0:3]
    weights = group_block[6]
    width = min(512, CAP)
    block_count = (live_count + width - 1) // width

    def row_step(row_block, result):
        row_start = row_block * width
        near = lax.dynamic_slice_in_dim(coords, row_start, width, 1)
        row_ids = row_start + jnp.arange(width, dtype=jnp.int32)

        def column_step(column_block, accum):
            column_start = column_block * width
            other = lax.dynamic_slice_in_dim(coords, column_start, width, 1)
            other_mass = lax.dynamic_slice_in_dim(weights, column_start, width, 0)
            column_ids = column_start + jnp.arange(width, dtype=jnp.int32)
            dist_sq = jnp.sum((near[:, :, None] - other[:, None, :]) ** 2, axis=0)
            inverse = jnp.where(
                row_ids[:, None] == column_ids[None, :], 0.0, lax.rsqrt(dist_sq + softening_sq)
            )
            return accum + jnp.sum(inverse * other_mass[None, :], axis=1)

        accum = lax.fori_loop(0, block_count, column_step, jnp.zeros((width,), jnp.float32))
        return lax.dynamic_update_slice_in_dim(result, -accum / CAP, row_start, 0)

    return lax.fori_loop(0, block_count, row_step, jnp.zeros((CAP,), jnp.float32))


def owner_work(received):
    items = received.shape[0]
    member_ranks = received[:, 7, :]
    valid = member_ranks >= 0.0
    target = jnp.where(valid, member_ranks.astype(jnp.int32), CAP)
    compact = (
        jnp.zeros((items, 7, CAP), jnp.float32)
        .at[jnp.arange(items)[:, None, None], jnp.arange(7)[None, :, None], target[:, None, :]]
        .set(received[:, 0:7, :], mode="drop")
    )
    live = jnp.sum(valid, axis=1, dtype=jnp.int32)
    pot = lax.map(lambda packed: potential_of(packed[0], packed[1]), (compact, live))
    weights = compact[:, 6, :]
    mass_sum = jnp.sum(weights, axis=1)
    bulk = jnp.sum(weights[:, None, :] * compact[:, 3:6, :], axis=2) / mass_sum[:, None]
    energy = 0.5 * jnp.sum((compact[:, 3:6, :] - bulk[:, :, None]) ** 2, axis=1) + pot
    both = jnp.stack([pot, energy], axis=1)
    safe = jnp.broadcast_to(jnp.minimum(target, CAP - 1)[:, None, :], (items, 2, target.shape[1]))
    answers = jnp.where(valid[:, None, :], jnp.take_along_axis(both, safe, axis=2), 0.0)
    stats = jnp.concatenate([mass_sum[:, None] / CAP, bulk], axis=1)
    return (answers, stats)


def shards(positions, velocities, masses, labels, owner_slot, group_cap):
    label_flat = labels[:, 0]
    count_dev = label_flat.shape[0]
    ngroups = owner_slot.shape[0]
    devices = lax.axis_size(("gx", "gy"))
    owned = ngroups // devices
    most_rows = 2 * count_dev // ngroups
    width_all = devices * most_rows
    row_width = min(512, count_dev)
    row_blocks = count_dev // row_width
    group_ids = jnp.arange(ngroups, dtype=jnp.int32)
    particle_ids = jnp.arange(count_dev, dtype=jnp.int32)
    block_starts = jnp.arange(row_blocks, dtype=jnp.int32) * row_width

    def tally(row_start):
        rows_label = lax.dynamic_slice_in_dim(label_flat, row_start, row_width, 0)
        rows_ids = row_start + jnp.arange(row_width, dtype=jnp.int32)
        same = (rows_label[:, None] == label_flat[None, :]) & (
            particle_ids[None, :] < rows_ids[:, None]
        )
        earlier = jnp.sum(same, axis=1, dtype=jnp.int32)
        hits = jnp.sum(rows_label[:, None] == group_ids[None, :], axis=0, dtype=jnp.int32)
        return (earlier, hits)

    earlier, hits = lax.map(tally, block_starts)
    local_rank = earlier.reshape(count_dev)
    counts = jnp.sum(hits, axis=0, dtype=jnp.int32)
    table = lax.all_gather(counts[None, :], ("gx", "gy"), axis=0, tiled=True)
    position = lax.axis_index(("gx", "gy"))
    below = (jnp.arange(devices, dtype=jnp.int32) < position)[:, None]
    prefix = jnp.sum(jnp.where(below, table, 0), axis=0, dtype=jnp.int32)
    totals = jnp.sum(table, axis=0, dtype=jnp.int32)
    limits = jnp.minimum(group_cap, CAP)
    kept_counts = jnp.minimum(totals, limits)
    starts = jnp.cumsum(kept_counts) - kept_counts
    lookup = jnp.stack([prefix, limits, starts, owner_slot], axis=1).astype(jnp.float32)

    def fetch(row_start):
        rows_label = lax.dynamic_slice_in_dim(label_flat, row_start, row_width, 0)
        onehot = (rows_label[:, None] == group_ids[None, :]).astype(jnp.float32)
        return jnp.dot(
            onehot, lookup, precision=lax.Precision.HIGHEST, preferred_element_type=jnp.float32
        )

    fetched = lax.map(fetch, block_starts).reshape(count_dev, 4).astype(jnp.int32)
    global_rank = fetched[:, 0] + local_rank
    keep = global_rank < fetched[:, 1]
    compact_index = jnp.where(keep, fetched[:, 2] + global_rank, -1)
    owner = fetched[:, 3] // owned
    local_group = fetched[:, 3] % owned
    dest = jnp.where(keep, owner * most_rows + local_rank, width_all)
    fields = jnp.concatenate(
        [positions, velocities, masses[None, :], global_rank.astype(jnp.float32)[None, :]], axis=0
    )
    outgoing = jnp.zeros((owned, 8, width_all), jnp.float32).at[:, 7, :].set(-1.0)
    outgoing = outgoing.at[local_group[:, None], jnp.arange(8)[None, :], dest[:, None]].set(
        jnp.transpose(fields), mode="drop"
    )
    answers, stats = owner_work(
        lax.all_to_all(outgoing, ("gx", "gy"), split_axis=2, concat_axis=2, tiled=True)
    )
    returned, stats = (
        lax.all_to_all(answers, ("gx", "gy"), split_axis=2, concat_axis=2, tiled=True),
        stats,
    )
    safe_dest = jnp.minimum(dest, width_all - 1)
    values = returned[local_group, :, safe_dest]
    potential = jnp.where(keep, values[:, 0], 0.0)
    binding = jnp.where(keep, values[:, 1], 0.0)
    catalog = jnp.transpose(stats)
    return (compact_index, potential, binding, catalog)


def solution(mesh):
    return jax.shard_map(
        shards,
        mesh=mesh,
        in_specs=(
            P(None, ("gx", "gy")),
            P(None, ("gx", "gy")),
            P(("gx", "gy")),
            P(("gx", "gy"), None),
            P(),
            P(),
        ),
        out_specs=(P(("gx", "gy")), P(("gx", "gy")), P(("gx", "gy")), P(None, ("gx", "gy"))),
        check_vma=False,
    )
```

profile of v0, /device:TPU:0, one launch (start us, length us, event | category | flops | bytes accessed | tf_op | source)
XLA Modules:
  0.0 391.8 jit_solution(1087029856079882510)
XLA Ops:
  0.7 23.5 %while.85 = (s32[]{:T(128)}, s32[4,512]{1,0:T(4,128)S(1)}, s32[4,256]{1,0:T(4,128)S(1)}, s32[4]{0:T(128)S(1)}, s32[2048]{0:T(1024)}, /*index=5*/s32[2048,1]{0,1:T(1,128)}, s32[]{:T(128)}, s32[]{:T(128)}, s32[]{:T(128)}) while((s32[]{:T(128)}, s32[4,512]{1,0:T(4,128)S(1)}, s32[4,256]{1,0:T(4,128)S(1)}, s32[4]{0:T(128)S(1)}, ...), condition=%wide.region_3.4_spmd.clone, body=%wide.region_0.3_spmd.clone.sunk | while | flops 5635845 | bytes 29851 | solution.py:87
  4.7 1.7 convert_reduce_fusion.5
  10.5 1.7 convert_reduce_fusion.5
  16.4 1.7 convert_reduce_fusion.5
  22.3 1.7 convert_reduce_fusion.5
  24.2 43.3 %all-gather.1 = s32[32,1,256]{2,1,0:T(1,128)S(1)} all-gather(s32[1,1,256]{2,1,0:T(1,128)S(1)} %bitcast.143), channel_id=2, replica_groups=mesh['gx'=8,'gy'=4] {'gx','gy'}, dimensions={0}, use_global_device_ids=true | all-gather | bytes 33792 | tf_op jit(solution)/shard_map/all_gather | solution.py:90
  70.4 14.8 %while.86 = (s32[]{:T(128)}, f32[4,512,4]{1,2,0:T(4,128)S(1)}, s32[4]{0:T(128)S(1)}, s32[2048]{0:T(1024)}, f32[256,4]{0,1:T(4,128)S(1)}, /*index=5*/s32[]{:T(128)}, s32[]{:T(128)}, s32[]{:T(128)}) while((s32[]{:T(128)}, f32[4,512,4]{1,2,0:T(4,128)S(1)}, s32[4]{0:T(128)S(1)}, s32[2048]{0:T(1024)}, f32[256,4]{0,1:T(4,128)S(1)}, ...), condition=%wide.region_10.11_spmd.clone, body=%wide.region_9.10_spmd.clone.sunk | while | flops 6422533 | bytes 18571 | solution.py:107
  88.1 60.4 %scatter_fusion = f32[32768]{0:T(1024)S(1)} fusion(f32[32768]{0:T(1024)S(1)} %copy-done, s32[16384]{0:T(1024)S(1)} %reshape.207, f32[16384]{0:T(1024)S(1)} %reshape.209), kind=kCustom, calls=%fused_computation.2 | custom fusion | bytes 262144
  149.3 1.7 reshape.228
  151.0 2.6 all-to-all-start
  153.6 8.2 %all-to-all-done = f32[32,1,1024]{2,1,0:T(1,128)S(1)} async-done(((f32[32,1,1024]{2,1,0:T(1,128)}), f32[32,1,1024]{2,1,0:T(1,128)S(1)}, u32[]{:S(2)}, u32[]{:S(2)}) %all-to-all-start) | async-done | bytes 131104 | tf_op jit(solution)/shard_map/all_to_all | solution.py:122
  163.3 1.1 reshape.229
  164.4 2.0 slice.103
  166.4 2.2 copy.44
  170.0 105.5 %scatter_custom_fusion.1 = f32[114688]{0:T(1024)S(1)} fusion(s32[28672]{0:T(1024)S(1)} %reshape.213, f32[28672]{0:T(1024)S(1)} %reshape.215, f32[]{:T(128)} %constant.240.clone.1), kind=kCustom, calls=%fused_computation.33 | custom fusion | bytes 458756
  276.0 20.6 %while.84 = (s32[]{:T(128)}, f32[8,2048]{1,0:T(8,128)S(1)}, s32[8]{0:T(128)S(1)}, f32[8,7,2048]{2,0,1:T(8,128)S(1)}, s32[]{:T(128)}, /*index=5*/s32[]{:T(128)}, ...) while((s32[]{:T(128)}, f32[8,2048]{1,0:T(8,128)S(1)}, ...), condition=%wide.region_21.22_spmd, body=%wide.region_14.21_spmd.sunk | while | flops 3409951 | bytes 2302925 | solution.py:51
  277.3 1.0 while.87
  282.5 1.0 while.87
  296.6 63.1 %gather_fusion.1 = f32[8192]{0:T(1024)S(1)} fusion(f32[8,2,2048]{2,0,1:T(8,128)S(1)} %pad_maximum_fusion, s32[8192]{0:T(1024)S(1)} %bitcast.106), kind=kCustom, calls=%fused_computation.1 | custom fusion | bytes 163840 | tf_op jit(solution)/shard_map/jit(take_along_axis)/gather | solution.py:58
  360.0 1.4 reshape.230
  361.4 2.6 all-to-all-start.1
  364.6 6.7 %all-to-all-done.1 = f32[32,1,256]{2,1,0:T(1,128)S(1)} async-done(((f32[32,1,256]{2,1,0:T(1,128)}), f32[32,1,256]{2,1,0:T(1,128)S(1)}, u32[]{:S(2)}, u32[]{:S(2)}) %all-to-all-start.1) | async-done | bytes 32800 | tf_op jit(solution)/shard_map/all_to_all | solution.py:125
  372.8 3.3 copy.41
  376.0 13.0 %gather_fusion = f32[2048,2]{1,0:T(8,128)S(1)} fusion(f32[8,2,512]{1,2,0:T(8,128)S(1)} %copy.41, s32[2048]{0:T(1024)S(1)} %bitcast.107), kind=kCustom, calls=%fused_computation | custom fusion | bytes 49152 | tf_op jit(solution)/shard_map/gather | solution.py:129
  (255 shorter events, 57.5 us)
Async XLA Ops:
  0.6 85.6 %copy-start.5 = (s32[3]{0:T(128)S(1)}, s32[3]{0:T(128)}, u32[]{:S(2)}) copy-start(s32[3]{0:T(128)} %constant.262) | copy-start | bytes 40
  70.3 16.9 %copy-start.1 = (f32[3,2048]{1,0:T(4,128)S(1)}, f32[3,2048]{1,0:T(4,128)}, u32[]{:S(2)}) copy-start(f32[3,2048]{1,0:T(4,128)} %param.19) | copy-start | bytes 73732
  70.4 16.9 %copy-start.2 = (f32[3,2048]{1,0:T(4,128)S(1)}, f32[3,2048]{1,0:T(4,128)}, u32[]{:S(2)}) copy-start(f32[3,2048]{1,0:T(4,128)} %param.18) | copy-start | bytes 73732
  70.4 16.9 %copy-start.3 = (f32[2048]{0:T(1024)S(1)}, f32[2048]{0:T(1024)}, u32[]{:S(2)}) copy-start(f32[2048]{0:T(1024)} %param.20) | copy-start | bytes 24580
  86.7 1.4 copy-start
  151.0 10.8 %all-to-all-start = ((f32[32,1,1024]{2,1,0:T(1,128)}), f32[32,1,1024]{2,1,0:T(1,128)S(1)}, u32[]{:S(2)}, u32[]{:S(2)}) async-start(f32[32,1,1024]{2,1,0:T(1,128)} %reshape.228), calls=%async_computation | async-start | bytes 262144 | tf_op jit(solution)/shard_map/all_to_all | solution.py:122
  166.4 2.5 copy-start.6
  166.4 2.6 copy-start.4
  361.4 9.8 %all-to-all-start.1 = ((f32[32,1,256]{2,1,0:T(1,128)}), f32[32,1,256]{2,1,0:T(1,128)S(1)}, u32[]{:S(2)}, u32[]{:S(2)}) async-start(f32[32,1,256]{2,1,0:T(1,128)} %reshape.230), calls=%async_computation.1 | async-start | bytes 65536 | tf_op jit(solution)/shard_map/all_to_all | solution.py:125
where the time goes:
time: 393 us; the launch traced here: 392 us
  local copies, waits for them, and re-layouts  279 us (71%)
  blocking collectives  43.3 us (11%)
  other arithmetic  25.1 us (6%)
  loops' own time  22.2 us (6%)
  waiting for transfers between devices  14.9 us (4%)
  starting transfers between devices  5.13 us (1%)
    unnamed x29, local copies, waits for them, and re-layouts  174 us
    gather x2, local copies, waits for them, and re-layouts, owner_work(): jnp.take_along_axis(both, safe, axis=2)  63.1 us
    all_gather x1, blocking collectives, shards(): table = lax.all_gather(counts[None, :], ('gx', 'gy'), axis=0, tiled=True)  43.3 us
    gather x1, local copies, waits for them, and re-layouts, shards(): values = returned[local_group, :, safe_dest]  13 us
    all_to_all x1, waiting for transfers between devices, shards(): lax.all_to_all(outgoing, ('gx', 'gy'), split_axis=2, concat_axis=2, tiled...  8.18 us
    another operation x1, loops' own time, shards(): earlier, hits = lax.map(tally, block_starts)  7.87 us
  transfers between devices with their start and end apart: 2, of which 2 were waited for; matrix products, arithmetic and copies ran while one was open for 0% of the time, Pallas kernels for 0%

commit v1 on v0

v1 whole, which is shorter than its diff:
```python
import functools

import jax
import jax.numpy as jnp
from jax import lax
from jax.experimental import pallas as pl
from jax.experimental.pallas import tpu as pltpu
from jax.sharding import PartitionSpec as P

CAP = 2048
LANES = 128
CHUNK = 256
CODE = 64
FIELDS = 7
softening_sq = 0.0025
F32 = jnp.float32
BF16 = jnp.bfloat16


def iota(shape, axis):
    return lax.broadcasted_iota(jnp.int32, shape, axis)


def parts_of(x):
    high = x.astype(BF16).astype(F32)
    rest = x - high
    middle = rest.astype(BF16).astype(F32)
    return high, middle, rest - middle


def inverse_column(owner_row, slots):
    groups = owner_row.shape[1]
    ids = iota((groups, groups), 1).astype(F32)
    return jnp.sum(jnp.where(owner_row == slots, ids, 0.0), axis=1, keepdims=True)


def send_kernel(devices, owned, label_ref, owner_ref, pos_ref, vel_ref, mass_ref, out_ref, code_ref):
    count = label_ref.shape[1]
    groups = devices * owned
    span = LANES // owned
    chunks = count // CHUNK
    rows = iota((groups, 1), 0)
    inverse = inverse_column(owner_ref[...], rows)
    upto = (iota((CHUNK, CHUNK), 0) <= iota((CHUNK, CHUNK), 1)).astype(F32).astype(BF16)
    base = jnp.broadcast_to((rows * CODE).astype(F32), (groups, CHUNK))
    owner_ids = iota((devices, 1, 1), 0)
    places = iota((LANES, 1), 0)
    total = jnp.zeros((devices * 8, LANES), F32)
    for chunk in range(chunks):
        cols = slice(chunk * CHUNK, (chunk + 1) * CHUNK)
        label = label_ref[:, cols].astype(F32)
        hit = label == inverse
        prefix = jnp.dot(jnp.where(hit, 1.0, 0.0).astype(BF16), upto, preferred_element_type=F32)
        value = jnp.sum(jnp.where(hit, prefix + base, 0.0), axis=0, keepdims=True)
        base = base + prefix[:, CHUNK - 1 : CHUNK]
        code = value.astype(jnp.int32) - 1
        slot = code // CODE
        rank = code % CODE
        owner = slot // owned
        local = slot % owned
        code_ref[:, cols] = (local * devices + owner) * CODE + rank
        place = local * span + rank
        picked = jnp.where(place == places, 1.0, 0.0).astype(BF16)
        fields = jnp.concatenate(
            [pos_ref[:, cols], vel_ref[:, cols], mass_ref[:, cols], jnp.zeros((1, CHUNK), F32)], axis=0
        )
        mine = owner[None] == owner_ids
        for part in parts_of(fields):
            spread = jnp.where(mine, part[None], 0.0).reshape(devices * 8, CHUNK).astype(BF16)
            total = total + lax.dot_general(
                spread, picked, (((1,), (1,)), ((), ())), preferred_element_type=F32
            )
    for device in range(devices):
        out_ref[device * FIELDS : (device + 1) * FIELDS, :] = total[device * 8 : device * 8 + FIELDS]


def owner_kernel(devices, owned, me_ref, got_ref, owner_ref, cap_ref, out_ref, stats_ref):
    span = LANES // owned
    blocks = devices // 8
    lane = iota((1, LANES), 1)
    offset = lane % span
    segment = lane // span

    def spin(x):
        return jnp.where(offset >= 1, pltpu.roll(x, 1, 1), pltpu.roll(x, LANES + 1 - span, 1))

    field = [got_ref[pl.ds(f, devices, stride=FIELDS), :] for f in range(FIELDS)]
    mass = field[6]
    valid = mass > 0.0

    slots = me_ref[0, 0] * owned + iota((owned, 1), 0)
    limit_col = jnp.sum(
        jnp.where(owner_ref[...] == slots, jnp.minimum(cap_ref[...], CAP).astype(F32), 0.0),
        axis=1,
        keepdims=True,
    )
    limit = jnp.sum(jnp.where(segment == iota((owned, 1), 0), limit_col, 0.0), axis=0, keepdims=True)

    joined = (iota((LANES, 1), 0) // span == segment).astype(F32).astype(BF16)
    counts = jnp.dot(jnp.where(valid, 1.0, 0.0).astype(BF16), joined, preferred_element_type=F32)
    before = (iota((devices, devices), 1) < iota((devices, devices), 0)).astype(F32).astype(BF16)
    prefix = jnp.dot(before, counts.astype(BF16), preferred_element_type=F32)
    kept = jnp.minimum(jnp.sum(counts, axis=0, keepdims=True), limit)
    keep = valid & (prefix + offset.astype(F32) < limit)
    mass = jnp.where(keep, mass, 0.0)

    sums = jnp.concatenate(
        [jnp.sum(x, axis=0, keepdims=True) for x in (mass, mass * field[3], mass * field[4], mass * field[5])]
        + [jnp.zeros((4, LANES), F32)],
        axis=0,
    )
    turned = sums
    for _ in range(span - 1):
        turned = spin(turned)
        sums = sums + turned
    mass_sum = sums[0:1]
    bulk = sums[1:4] / mass_sum
    stats = jnp.concatenate([mass_sum / CAP, bulk, jnp.zeros((4, LANES), F32)], axis=0)
    columns = iota((1, owned), 1)
    table = jnp.zeros((8, owned), F32)
    for group in range(owned):
        table = jnp.where(columns == group, stats[:, group * span : group * span + 1], table)
    stats_ref[...] = table[0:4]

    near = [[x[b * 8 : b * 8 + 8] for b in range(blocks)] for x in (field[0], field[1], field[2], mass)]

    def pair_block(turned, diagonal, one_way, off_diagonal, acc):
        acc = list(acc)
        far_sum = [None] * blocks
        for shift in range(8):
            on_diag = shift in diagonal
            single = shift in one_way
            for b in range(blocks):
                others = list(range(b)) if off_diagonal else []
                if on_diag or single:
                    others.append(b)
                if not others:
                    continue
                far = [turned[k * blocks + b] for k in range(4)]
                if shift:
                    far = [pltpu.roll(x, 8 - shift, 0) for x in far]
                back = None
                for a in others:
                    dx = near[0][a] - far[0]
                    dy = near[1][a] - far[1]
                    dz = near[2][a] - far[2]
                    inverse = lax.rsqrt((dx * dx + dy * dy) + (dz * dz + softening_sq))
                    acc[a] = acc[a] + far[3] * inverse
                    if a == b and single:
                        continue
                    term = near[3][a] * inverse
                    back = term if back is None else back + term
                if back is not None:
                    if shift:
                        back = pltpu.roll(back, shift, 0)
                    far_sum[b] = back if far_sum[b] is None else far_sum[b] + back
        far_sum = [jnp.zeros((8, LANES), F32) if x is None else x for x in far_sum]
        return acc, far_sum

    half = span // 2
    every = tuple(range(8))
    flat = [near[k][b] for k in range(4) for b in range(blocks)]
    zeros = [jnp.zeros((8, LANES), F32)] * blocks

    def turn(diagonal, one_way, _, carry):
        turned, acc, far = carry
        turned = [spin(x) for x in turned]
        acc, extra = pair_block(turned, diagonal, one_way, True, acc)
        far = [spin(x + y) for x, y in zip(far, extra)]
        return turned, acc, far

    carry = (flat, zeros, zeros)
    carry = lax.fori_loop(half + 1, span, functools.partial(turn, (), ()), carry)
    carry = turn((1, 2, 3), (0, 4), 0, carry)
    carry = lax.fori_loop(1, half, functools.partial(turn, every, ()), carry)
    _, acc, far = carry
    acc, extra = pair_block(flat, (1, 2, 3), (4,), True, acc)
    pot = jnp.concatenate([x + (y + z) for x, y, z in zip(acc, far, extra)], axis=0) / -CAP

    wide = functools.partial(jnp.broadcast_to, shape=(devices, LANES))
    more = jnp.where(offset == 3, prefix, wide(kept))
    for axis in range(3):
        more = jnp.where(offset == axis, wide(bulk[axis : axis + 1]), more)
    out_ref[pl.ds(0, devices, stride=2), :] = pot
    out_ref[pl.ds(1, devices, stride=2), :] = more


def final_kernel(
    devices, owned, code_ref, label_ref, owner_ref, vel_ref, got_ref, index_ref, pot_ref, bind_ref
):
    count = code_ref.shape[1]
    groups = devices * owned
    span = LANES // owned
    lane = iota((1, LANES), 1)
    rows = iota((groups, 1), 0)
    inverse = inverse_column(owner_ref[...], (rows % devices) * owned + rows // devices)
    pots = got_ref[pl.ds(0, devices, stride=2), :]
    more = got_ref[pl.ds(1, devices, stride=2), :]
    table = []
    for group in range(owned):
        left = pots if group == 0 else pltpu.roll(pots, LANES - group * span, 1)
        right = pltpu.roll(more, (LANES + span - group * span) % LANES, 1) if group != 1 else more
        table.append(jnp.where(lane < span, left, right))
    table = jnp.transpose(jnp.concatenate(table, axis=0))[0 : 2 * span]
    parts = jnp.concatenate(parts_of(table), axis=0).astype(BF16)
    used = 2 * span
    kept_row = 2 * span - 1
    for chunk in range(count // CHUNK):
        cols = slice(chunk * CHUNK, (chunk + 1) * CHUNK)
        code = code_ref[:, cols]
        rank = code % CODE
        hit = jnp.where(code // CODE == rows, 1.0, 0.0).astype(BF16)
        lower = jnp.where(inverse < label_ref[:, cols].astype(F32), 1.0, 0.0).astype(BF16)
        found = jnp.dot(parts, hit, preferred_element_type=F32)
        found = (found[0:used] + found[used : 2 * used]) + found[2 * used :]
        starts = jnp.dot(parts, lower, preferred_element_type=F32)
        start = starts[kept_row : kept_row + 1] + starts[used + kept_row : used + kept_row + 1]
        pot = jnp.sum(jnp.where(iota((span, 1), 0) == rank, found[0:span], 0.0), axis=0, keepdims=True)
        prefix = found[span + 3 : span + 4]
        kept = found[kept_row : kept_row + 1]
        global_rank = prefix + rank.astype(F32)
        keep = global_rank < kept
        speed = jnp.sum((vel_ref[:, cols] - found[span : span + 3]) ** 2, axis=0, keepdims=True)
        index_ref[:, cols] = jnp.where(keep, (start + global_rank).astype(jnp.int32), -1)
        pot_ref[:, cols] = jnp.where(keep, pot, 0.0)
        bind_ref[:, cols] = jnp.where(keep, 0.5 * speed + pot, 0.0)


def shards(positions, velocities, masses, labels, owner_slot, group_cap):
    count = labels.shape[0]
    groups = owner_slot.shape[0]
    devices = lax.axis_size(("gx", "gy"))
    owned = groups // devices
    label_row = labels.reshape(1, count)
    owner_row = owner_slot.reshape(1, groups)
    cap_row = group_cap.reshape(1, groups)
    me = lax.axis_index(("gx", "gy")).astype(jnp.int32).reshape(1, 1)
    params = pltpu.CompilerParams(vmem_limit_bytes=60 * 1024 * 1024)

    def exchange(x, rows):
        flat = x.reshape(devices * rows * LANES)
        flat = lax.all_to_all(flat, ("gx", "gy"), split_axis=0, concat_axis=0, tiled=True)
        return flat.reshape(devices * rows, LANES)

    outgoing, code = pl.pallas_call(
        functools.partial(send_kernel, devices, owned),
        out_shape=(
            jax.ShapeDtypeStruct((devices * FIELDS, LANES), F32),
            jax.ShapeDtypeStruct((1, count), jnp.int32),
        ),
        compiler_params=params,
        name="send",
    )(label_row, owner_row, positions, velocities, masses.reshape(1, count))
    received = exchange(outgoing, FIELDS)
    answers, catalog = pl.pallas_call(
        functools.partial(owner_kernel, devices, owned),
        out_shape=(
            jax.ShapeDtypeStruct((devices * 2, LANES), F32),
            jax.ShapeDtypeStruct((4, owned), F32),
        ),
        in_specs=[pl.BlockSpec(memory_space=pltpu.SMEM)] + [pl.BlockSpec(memory_space=pltpu.VMEM)] * 3,
        compiler_params=params,
        name="owner",
    )(me, received, owner_row, cap_row)
    returned = exchange(answers, 2)
    index, potential, binding = pl.pallas_call(
        functools.partial(final_kernel, devices, owned),
        out_shape=(
            jax.ShapeDtypeStruct((1, count), jnp.int32),
            jax.ShapeDtypeStruct((1, count), F32),
            jax.ShapeDtypeStruct((1, count), F32),
        ),
        compiler_params=params,
        name="final",
    )(code, label_row, owner_row, velocities, returned)
    return index.reshape(count), potential.reshape(count), binding.reshape(count), catalog


def solution(mesh):
    return jax.shard_map(
        shards,
        mesh=mesh,
        in_specs=(
            P(None, ("gx", "gy")),
            P(None, ("gx", "gy")),
            P(("gx", "gy")),
            P(("gx", "gy"), None),
            P(),
            P(),
        ),
        out_specs=(P(("gx", "gy")), P(("gx", "gy")), P(("gx", "gy")), P(None, ("gx", "gy"))),
        check_vma=False,
    )
```

time: 393 us -> 41.2 us (0.10)
  local copies, waits for them, and re-layouts: 279 us -> 0.64 us
  blocking collectives: 43.3 us -> 10.4 us
  other arithmetic: 25.1 us -> 0 us
  loops' own time: 22.2 us -> 0 us
  Pallas kernels: 0 us -> 13.8 us
  waiting for transfers between devices: 14.9 us -> 7.99 us
    unnamed x29 -> x2, local copies, waits for them, and re-layouts: 174 us -> 0.64 us
    gather x3 -> x0, local copies, waits for them, and re-layouts: 76.2 us -> none  [the longest x2 63.1 us: owner_work(): jnp.take_along_axis(both, safe, axis=2)]
    all_gather x1 -> x0, blocking collectives: 43.3 us -> none  [shards(): table = lax.all_gather(counts[None, :], ('gx', 'gy'), axis=0, tiled=True)]
    another operation x19 -> x0, loops' own time: 22.2 us -> none  [the longest x1 7.87 us: shards(): earlier, hits = lax.map(tally, block_starts)]
    dynamic_slice x48 -> x0, local copies, waits for them, and re-layouts: 16.4 us -> none  [the longest x8 4.79 us: shards(): earlier, hits = lax.map(tally, block_starts)]
    pallas_call x0 -> x3, Pallas kernels: none -> 13.8 us  [the longest x1 7.33 us: shards(): pl.pallas_call(functools.partial(owner_kernel, devices, owned), out_shape...]
    reduce_sum x30 -> x0, other arithmetic: 13.2 us -> none  [the longest x4 6.66 us: tally(): earlier = jnp.sum(same, axis=1, dtype=jnp.int32)]
    all_to_all x0 -> x1, blocking collectives: none -> 10.4 us  [exchange(): lax.all_to_all(flat, ('gx', 'gy'), split_axis=0, concat_axis=0, tiled=True)]
  transfers between devices with their start and end apart: 2 -> 1, of which waited for: 2 -> 1; matrix products, arithmetic and copies ran while one was open for 0% -> 0% of each run, Pallas kernels for 0% -> 0%
where the time goes in v1:
time: 41.2 us; the launch traced here: 40.8 us
  Pallas kernels  13.8 us (33%)
  blocking collectives  10.4 us (25%)
  waiting for transfers between devices  7.99 us (19%)
  starting transfers between devices  7.32 us (18%)
  between operations  0.65 us (2%)
  local copies, waits for them, and re-layouts  0.64 us (2%)
    all_to_all x1, blocking collectives, exchange(): lax.all_to_all(flat, ('gx', 'gy'), split_axis=0, concat_axis=0, tiled=True)  10.4 us
    all_to_all x1, waiting for transfers between devices, exchange(): lax.all_to_all(flat, ('gx', 'gy'), split_axis=0, concat_axis=0, tiled=True)  7.99 us
    pallas_call x1, Pallas kernels, shards(): pl.pallas_call(functools.partial(owner_kernel, devices, owned), out_shape...  7.33 us
    all_to_all x1, starting transfers between devices, exchange(): lax.all_to_all(flat, ('gx', 'gy'), split_axis=0, concat_axis=0, tiled=True)  7.32 us
    pallas_call x1, Pallas kernels, shards(): pl.pallas_call(functools.partial(send_kernel, devices, owned), out_shape=...  4.27 us
    pallas_call x1, Pallas kernels, shards(): pl.pallas_call(functools.partial(final_kernel, devices, owned), out_shape...  2.17 us
  transfers between devices with their start and end apart: 1, of which 1 were waited for; matrix products, arithmetic and copies ran while one was open for 0% of the time, Pallas kernels for 0%

profile of v1, /device:TPU:0, one launch (start us, length us, event | category | flops | bytes accessed | tf_op | source)
XLA Modules:
  0.0 40.8 jit_solution(1027188437016523582)
XLA Ops:
  0.6 4.3 %send.1 = (f32[224,128]{1,0:T(8,128)}, s32[1,2048]{1,0:T(1,128)}) custom-call(s32[1,2048]{1,0:T(1,128)} %bitcast.16, s32[1,256]{1,0:T(1,128)} %bitcast.18, f32[3,2048]{1,0:T(4,128)} %pos_ref.1, f32[3,2048]{1,0:T(4,128)} %vel_ref.3, f32[1,2048]{1,0:T(1,128)} %bitcast.21), custom_call_target="tpu_custom_call" | custom-call | tf_op jit(solution)/shard_map/send/pallas_call | solution.py:245
  4.9 7.3 %all-to-all-start = ((f32[32,896,1]{1,2,0:T(1,128)}), f32[32,896,1]{1,2,0:T(1,128)S(1)}, u32[]{:S(2)}, u32[]{:S(2)}) async-start(f32[32,896,1]{1,2,0:T(1,128)} %bitcast.14), calls=%async_computation | async-start | bytes 229376 | tf_op jit(solution)/shard_map/all_to_all | solution.py:242
  12.2 8.0 %all-to-all-done = f32[32,896,1]{1,2,0:T(1,128)S(1)} async-done(((f32[32,896,1]{1,2,0:T(1,128)}), f32[32,896,1]{1,2,0:T(1,128)S(1)}, u32[]{:S(2)}, u32[]{:S(2)}) %all-to-all-start) | async-done | bytes 114720 | tf_op jit(solution)/shard_map/all_to_all | solution.py:242
  20.2 0.0 copy-start
  20.2 0.6 %copy-done = f32[32,896,1]{1,2,0:T(1,128)} copy-done((f32[32,896,1]{1,2,0:T(1,128)}, f32[32,896,1]{1,2,0:T(1,128)S(1)}, u32[]{:S(2)}) %copy-start) | copy-done | bytes 114712
  20.9 7.3 %owner.1 = (f32[64,128]{1,0:T(8,128)}, f32[4,8]{1,0:T(4,128)}) custom-call(s32[1,1]{1,0:T(1,128)} %bitcast.3.me_ref, f32[224,128]{1,0:T(8,128)} %bitcast.12, s32[1,256]{1,0:T(1,128)} %bitcast.19, s32[1,256]{1,0:T(1,128)} %bitcast.22), custom_call_target="tpu_custom_call" | custom-call | tf_op jit(solution)/shard_map/owner/pallas_call | solution.py:255
  28.2 10.4 %all_to_all.18 = f32[32,256,1]{1,2,0:T(1,128)} all-to-all(f32[32,256,1]{1,2,0:T(1,128)} %bitcast.15), channel_id=1, replica_groups=mesh['gx'=8,'gy'=4] {'gx','gy'}, dimensions={0} | all-to-all | bytes 65536 | tf_op jit(solution)/shard_map/all_to_all | solution.py:242
  38.6 2.2 %final.1 = (s32[1,2048]{1,0:T(1,128)}, f32[1,2048]{1,0:T(1,128)}, f32[1,2048]{1,0:T(1,128)}) custom-call(s32[1,2048]{1,0:T(1,128)} %get-tuple-element.11.code_ref, s32[1,2048]{1,0:T(1,128)} %bitcast.17, s32[1,256]{1,0:T(1,128)} %bitcast.20, f32[3,2048]{1,0:T(4,128)} %vel_ref.3, f32[64,128]{1,0:T(8,128)} %bitcast.13), custom_call_target="tpu_custom_call" | custom-call | tf_op jit(solution)/shard_map/final/pallas_call | solution.py:266
Async XLA Ops:
  4.9 15.3 %all-to-all-start = ((f32[32,896,1]{1,2,0:T(1,128)}), f32[32,896,1]{1,2,0:T(1,128)S(1)}, u32[]{:S(2)}, u32[]{:S(2)}) async-start(f32[32,896,1]{1,2,0:T(1,128)} %bitcast.14), calls=%async_computation | async-start | bytes 229376 | tf_op jit(solution)/shard_map/all_to_all | solution.py:242
  20.2 0.6 %copy-start = (f32[32,896,1]{1,2,0:T(1,128)}, f32[32,896,1]{1,2,0:T(1,128)S(1)}, u32[]{:S(2)}) copy-start(f32[32,896,1]{1,2,0:T(1,128)S(1)} %all-to-all-done) | copy-start | bytes 344068

commit v2 on v1

--- a/solution.py
+++ b/solution.py
@@ -34,47 +34,98 @@
     return jnp.sum(jnp.where(owner_row == slots, ids, 0.0), axis=1, keepdims=True)
 
 
-def send_kernel(devices, owned, label_ref, owner_ref, pos_ref, vel_ref, mass_ref, out_ref, code_ref):
+def send_kernel(
+    devices, owned, me_ref, label_hbm, owner_hbm, cap_hbm, pos_hbm, vel_hbm, mass_hbm,
+    out_ref, code_ref, limit_ref, owner_out,
+    label_ref, owner_ref, cap_ref, pos_ref, vel_ref, mass_ref, parts_ref, hit_ref, spread_ref, block_ref, sems,
+):
     count = label_ref.shape[1]
     groups = devices * owned
     span = LANES // owned
-    chunks = count // CHUNK
+    shift = owned.bit_length() - 1
+    copies = [
+        pltpu.make_async_copy(source, target, sems.at[k])
+        for k, (source, target) in enumerate(
+            (
+                (owner_hbm, owner_ref),
+                (label_hbm, label_ref),
+                (pos_hbm, pos_ref),
+                (vel_hbm, vel_ref),
+                (mass_hbm, mass_ref),
+                (cap_hbm, cap_ref),
+            )
+        )
+    ]
+    for copy in copies:
+        copy.start()
     rows = iota((groups, 1), 0)
+    upto = (iota((CHUNK, CHUNK), 0) <= iota((CHUNK, CHUNK), 1)).astype(F32).astype(BF16)
+    copies[0].wait()
     inverse = inverse_column(owner_ref[...], rows)
-    upto = (iota((CHUNK, CHUNK), 0) <= iota((CHUNK, CHUNK), 1)).astype(F32).astype(BF16)
-    base = jnp.broadcast_to((rows * CODE).astype(F32), (groups, CHUNK))
-    owner_ids = iota((devices, 1, 1), 0)
-    places = iota((LANES, 1), 0)
-    total = jnp.zeros((devices * 8, LANES), F32)
-    for chunk in range(chunks):
+    owner_out[...] = owner_ref[...]
+    for copy in copies[1:]:
+        copy.wait()
+
+    slots = me_ref[0, 0] * owned + iota((owned, 1), 0)
+    limit_col = jnp.sum(
+        jnp.where(owner_ref[...] == slots, jnp.minimum(cap_ref[...], CAP).astype(F32), 0.0),
+        axis=1,
+        keepdims=True,
+    )
+    segment = iota((1, LANES), 1) // span
+    limit_ref[...] = jnp.sum(
+        jnp.where(segment == iota((owned, 1), 0), limit_col, 0.0), axis=0, keepdims=True
+    )
+
+    fields = jnp.concatenate([pos_ref[...], vel_ref[...], mass_ref[...], jnp.zeros((1, count), F32)], axis=0)
+    for k, part in enumerate(parts_of(fields)):
+        for chunk in range(count // CHUNK):
+            parts_ref[chunk * 24 + k * 8 : chunk * 24 + k * 8 + 8, :] = part[:, chunk * CHUNK : (chunk + 1) * CHUNK]
+        spread_ref[k * LANES + FIELDS * span : (k + 1) * LANES, :] = jnp.zeros((span, count), BF16)
+
+    base = jnp.broadcast_to((rows * CODE).astype(F32), (groups, LANES))
+    ranks = iota((span, 1), 0)
+    for chunk in range(count // CHUNK):
         cols = slice(chunk * CHUNK, (chunk + 1) * CHUNK)
-        label = label_ref[:, cols].astype(F32)
-        hit = label == inverse
-        prefix = jnp.dot(jnp.where(hit, 1.0, 0.0).astype(BF16), upto, preferred_element_type=F32)
-        value = jnp.sum(jnp.where(hit, prefix + base, 0.0), axis=0, keepdims=True)
+        hit = label_ref[:, cols].astype(F32) == inverse
+        packed = jnp.where(hit, 1.0, 0.0).astype(BF16)
+        hit_ref[:, cols] = packed
+        prefix = jnp.dot(packed, upto, preferred_element_type=F32)
+        wide = jnp.concatenate([base] * (CHUNK // LANES), axis=1)
+        value = jnp.sum(jnp.where(hit, prefix + wide, 0.0), axis=0, keepdims=True)
         base = base + prefix[:, CHUNK - 1 : CHUNK]
         code = value.astype(jnp.int32) - 1
-        slot = code // CODE
-        rank = code % CODE
-        owner = slot // owned
-        local = slot % owned
-        code_ref[:, cols] = (local * devices + owner) * CODE + rank
-        place = local * span + rank
-        picked = jnp.where(place == places, 1.0, 0.0).astype(BF16)
-        fields = jnp.concatenate(
-            [pos_ref[:, cols], vel_ref[:, cols], mass_ref[:, cols], jnp.zeros((1, CHUNK), F32)], axis=0
-        )
-        mine = owner[None] == owner_ids
-        for part in parts_of(fields):
-            spread = jnp.where(mine, part[None], 0.0).reshape(devices * 8, CHUNK).astype(BF16)
-            total = total + lax.dot_general(
-                spread, picked, (((1,), (1,)), ((), ())), preferred_element_type=F32
-            )
-    for device in range(devices):
-        out_ref[device * FIELDS : (device + 1) * FIELDS, :] = total[device * 8 : device * 8 + FIELDS]
-
-
-def owner_kernel(devices, owned, me_ref, got_ref, owner_ref, cap_ref, out_ref, stats_ref):
+        slot = code >> 6
+        rank = code & (CODE - 1)
+        code_ref[:, cols] = (((slot & (owned - 1)) * devices + (slot >> shift)) << 6) + rank
+        mine = rank == ranks
+        for k in range(3):
+            for f in range(FIELDS):
+                row = parts_ref[pl.ds(chunk * 24 + k * 8 + f, span, stride=0), :]
+                spread_ref[k * LANES + f * span : k * LANES + (f + 1) * span, cols] = jnp.where(
+                    mine, row, 0.0
+                ).astype(BF16)
+
+    found = lax.dot_general(
+        hit_ref[...], spread_ref[...], (((1,), (1,)), ((), ())), preferred_element_type=F32
+    )
+    block_ref[...] = (found[:, 0:LANES] + found[:, LANES : 2 * LANES]) + found[:, 2 * LANES :]
+    block = [block_ref[pl.ds(g, devices, stride=owned), :] for g in range(owned)]
+    step = owned // 2
+    while step:
+        upper = (segment & step) != 0
+        for low in range(owned):
+            if low & step:
+                continue
+            one, two = block[low], block[low + step]
+            block[low] = jnp.where(upper, pltpu.roll(two, step * span, 1), one)
+            block[low + step] = jnp.where(upper, two, pltpu.roll(one, LANES - step * span, 1))
+        step //= 2
+    for f in range(FIELDS):
+        out_ref[pl.ds(f, devices, stride=FIELDS), :] = block[f]
+
+
+def owner_kernel(devices, owned, got_ref, limit_ref, out_ref, stats_ref):
     span = LANES // owned
     blocks = devices // 8
     lane = iota((1, LANES), 1)
@@ -88,13 +139,7 @@
     mass = field[6]
     valid = mass > 0.0
 
-    slots = me_ref[0, 0] * owned + iota((owned, 1), 0)
-    limit_col = jnp.sum(
-        jnp.where(owner_ref[...] == slots, jnp.minimum(cap_ref[...], CAP).astype(F32), 0.0),
-        axis=1,
-        keepdims=True,
-    )
-    limit = jnp.sum(jnp.where(segment == iota((owned, 1), 0), limit_col, 0.0), axis=0, keepdims=True)
+    limit = limit_ref[...]
 
     joined = (iota((LANES, 1), 0) // span == segment).astype(F32).astype(BF16)
     counts = jnp.dot(jnp.where(valid, 1.0, 0.0).astype(BF16), joined, preferred_element_type=F32)
@@ -169,10 +214,16 @@
         far = [spin(x + y) for x, y in zip(far, extra)]
         return turned, acc, far
 
-    carry = (flat, zeros, zeros)
-    carry = lax.fori_loop(half + 1, span, functools.partial(turn, (), ()), carry)
+    def repeat(diagonal, carry):
+        if blocks > 4:
+            return lax.fori_loop(1, half, functools.partial(turn, diagonal, ()), carry)
+        for _ in range(1, half):
+            carry = turn(diagonal, (), 0, carry)
+        return carry
+
+    carry = repeat((), (flat, zeros, zeros))
     carry = turn((1, 2, 3), (0, 4), 0, carry)
-    carry = lax.fori_loop(1, half, functools.partial(turn, every, ()), carry)
+    carry = repeat(every, carry)
     _, acc, far = carry
     acc, extra = pair_block(flat, (1, 2, 3), (4,), True, acc)
     pot = jnp.concatenate([x + (y + z) for x, y, z in zip(acc, far, extra)], axis=0) / -CAP
@@ -202,22 +253,23 @@
         right = pltpu.roll(more, (LANES + span - group * span) % LANES, 1) if group != 1 else more
         table.append(jnp.where(lane < span, left, right))
     table = jnp.transpose(jnp.concatenate(table, axis=0))[0 : 2 * span]
-    parts = jnp.concatenate(parts_of(table), axis=0).astype(BF16)
+    parts = parts_of(table)
+    counted = jnp.concatenate([part[2 * span - 8 :] for part in parts[0:2]], axis=0).astype(BF16)
+    parts = jnp.concatenate(parts, axis=0).astype(BF16)
     used = 2 * span
-    kept_row = 2 * span - 1
     for chunk in range(count // CHUNK):
         cols = slice(chunk * CHUNK, (chunk + 1) * CHUNK)
         code = code_ref[:, cols]
-        rank = code % CODE
-        hit = jnp.where(code // CODE == rows, 1.0, 0.0).astype(BF16)
+        rank = code & (CODE - 1)
+        hit = jnp.where(code >> 6 == rows, 1.0, 0.0).astype(BF16)
         lower = jnp.where(inverse < label_ref[:, cols].astype(F32), 1.0, 0.0).astype(BF16)
         found = jnp.dot(parts, hit, preferred_element_type=F32)
         found = (found[0:used] + found[used : 2 * used]) + found[2 * used :]
-        starts = jnp.dot(parts, lower, preferred_element_type=F32)
-        start = starts[kept_row : kept_row + 1] + starts[used + kept_row : used + kept_row + 1]
+        starts = jnp.dot(counted, lower, preferred_element_type=F32)
+        start = starts[7:8] + starts[15:16]
         pot = jnp.sum(jnp.where(iota((span, 1), 0) == rank, found[0:span], 0.0), axis=0, keepdims=True)
         prefix = found[span + 3 : span + 4]
-        kept = found[kept_row : kept_row + 1]
+        kept = found[used - 1 : used]
         global_rank = prefix + rank.astype(F32)
         keep = global_rank < kept
         speed = jnp.sum((vel_ref[:, cols] - found[span : span + 3]) ** 2, axis=0, keepdims=True)
@@ -235,22 +287,44 @@
     owner_row = owner_slot.reshape(1, groups)
     cap_row = group_cap.reshape(1, groups)
     me = lax.axis_index(("gx", "gy")).astype(jnp.int32).reshape(1, 1)
-    params = pltpu.CompilerParams(vmem_limit_bytes=60 * 1024 * 1024)
+    params = pltpu.CompilerParams(vmem_limit_bytes=min(48, 8 * groups // 128) * 1024 * 1024)
 
     def exchange(x, rows):
         flat = x.reshape(devices * rows * LANES)
         flat = lax.all_to_all(flat, ("gx", "gy"), split_axis=0, concat_axis=0, tiled=True)
         return flat.reshape(devices * rows, LANES)
 
-    outgoing, code = pl.pallas_call(
+    outgoing, code, limit, owner_kept = pl.pallas_call(
         functools.partial(send_kernel, devices, owned),
         out_shape=(
             jax.ShapeDtypeStruct((devices * FIELDS, LANES), F32),
             jax.ShapeDtypeStruct((1, count), jnp.int32),
-        ),
+            jax.ShapeDtypeStruct((1, LANES), F32),
+            jax.ShapeDtypeStruct((1, groups), jnp.int32),
+        ),
+        in_specs=[pl.BlockSpec(memory_space=pltpu.SMEM)] + [pl.BlockSpec(memory_space=pltpu.HBM)] * 6,
+        scratch_shapes=[
+            pltpu.VMEM((1, count), jnp.int32),
+            pltpu.VMEM((1, groups), jnp.int32),
+            pltpu.VMEM((1, groups), jnp.int32),
+            pltpu.VMEM((3, count), F32),
+            pltpu.VMEM((3, count), F32),
+            pltpu.VMEM((1, count), F32),
+            pltpu.VMEM((24 * count // CHUNK, CHUNK), F32),
+            pltpu.VMEM((groups, count), BF16),
+            pltpu.VMEM((3 * LANES, count), BF16),
+            pltpu.VMEM((groups, LANES), F32),
+            pltpu.SemaphoreType.DMA((6,)),
+        ],
         compiler_params=params,
         name="send",
-    )(label_row, owner_row, positions, velocities, masses.reshape(1, count))
+    )(
+        me,
+        *(
+            pltpu.with_memory_space_constraint(x, pltpu.HBM)
+            for x in (label_row, owner_row, cap_row, positions, velocities, masses.reshape(1, count))
+        ),
+    )
     received = exchange(outgoing, FIELDS)
     answers, catalog = pl.pallas_call(
         functools.partial(owner_kernel, devices, owned),
@@ -258,10 +332,9 @@
             jax.ShapeDtypeStruct((devices * 2, LANES), F32),
             jax.ShapeDtypeStruct((4, owned), F32),
         ),
-        in_specs=[pl.BlockSpec(memory_space=pltpu.SMEM)] + [pl.BlockSpec(memory_space=pltpu.VMEM)] * 3,
         compiler_params=params,
         name="owner",
-    )(me, received, owner_row, cap_row)
+    )(received, limit)
     returned = exchange(answers, 2)
     index, potential, binding = pl.pallas_call(
         functools.partial(final_kernel, devices, owned),
@@ -272,7 +345,7 @@
         ),
         compiler_params=params,
         name="final",
-    )(code, label_row, owner_row, velocities, returned)
+    )(code, label_row, owner_kept, velocities, returned)
     return index.reshape(count), potential.reshape(count), binding.reshape(count), catalog
 
 

time: 41.2 us -> 31.5 us (0.76)
  blocking collectives: 10.4 us -> 24.2 us
  waiting for transfers between devices: 7.99 us -> 0 us
  Pallas kernels: 13.8 us -> 6.42 us
  starting transfers between devices: 7.32 us -> 0 us
  local copies, waits for them, and re-layouts: 0.64 us -> 0.01 us
    all_to_all x1 -> x2, blocking collectives: 10.4 us -> 24.2 us  [exchange(): lax.all_to_all(flat, ('gx', 'gy'), split_axis=0, concat_axis=0, tiled=True)]
    all_to_all x1 -> x0, waiting for transfers between devices: 7.99 us -> none  [exchange(): lax.all_to_all(flat, ('gx', 'gy'), split_axis=0, concat_axis=0, tiled=True)]
    all_to_all x1 -> x0, starting transfers between devices: 7.32 us -> none  [exchange(): lax.all_to_all(flat, ('gx', 'gy'), split_axis=0, concat_axis=0, tiled=True)]
    pallas_call x1, Pallas kernels: 7.33 us -> 2.9 us  [shards(): pl.pallas_call(functools.partial(owner_kernel, devices, owned), out_shape...]
    pallas_call x1, Pallas kernels: 4.27 us -> 2.27 us  [shards(): pl.pallas_call(functools.partial(send_kernel, devices, owned), out_shape=...]
    pallas_call x1, Pallas kernels: 2.17 us -> 1.25 us  [shards(): pl.pallas_call(functools.partial(final_kernel, devices, owned), out_shape...]
    unnamed x2 -> x4, local copies, waits for them, and re-layouts: 0.64 us -> 0.01 us
  transfers between devices with their start and end apart: 1 -> 0, of which waited for: 1 -> 0; matrix products, arithmetic and copies ran while one was open for 0% -> 0% of each run, Pallas kernels for 0% -> 0%
where the time goes in v2:
time: 31.5 us; the launch traced here: 31.3 us
  blocking collectives  24.2 us (77%)
  Pallas kernels  6.42 us (20%)
  between operations  0.65 us (2%)
    all_to_all x2, blocking collectives, exchange(): lax.all_to_all(flat, ('gx', 'gy'), split_axis=0, concat_axis=0, tiled=True)  24.2 us
    pallas_call x1, Pallas kernels, shards(): pl.pallas_call(functools.partial(owner_kernel, devices, owned), out_shape...  2.9 us
    pallas_call x1, Pallas kernels, shards(): pl.pallas_call(functools.partial(send_kernel, devices, owned), out_shape=...  2.27 us
    pallas_call x1, Pallas kernels, shards(): pl.pallas_call(functools.partial(final_kernel, devices, owned), out_shape...  1.25 us

profile of v2, /device:TPU:0, one launch (start us, length us, event | category | flops | bytes accessed | tf_op | source)
XLA Modules:
  0.0 31.3 jit_solution(3935834216695450562)
XLA Ops:
  0.6 2.3 %send.1 = (f32[224,128]{1,0:T(8,128)S(1)}, s32[1,2048]{1,0:T(1,128)S(1)}, f32[1,128]{1,0:T(1,128)S(1)}, s32[1,256]{1,0:T(1,128)S(1)}) custom-call(s32[1,1]{1,0:T(1,128)} %bitcast.me_ref, s32[1,2048]{1,0:T(1,128)} %bitcast.16, s32[1,256]{1,0:T(1,128)} %bitcast.19, s32[1,256]{1,0:T(1,128)} %bitcast.20, f32[3,2048]{1,0:T(4,128)} %pos_hbm.1, f32[3,2048]{1,0:T(4,128)} %vel_ref.1, ...), custom_call_target="tpu_custom_call" | custom-call | tf_op jit(solution)/shard_map/send/pallas_call | solution.py:297
  2.9 15.1 %all_to_all.18 = f32[32,896,1]{1,2,0:T(1,128)S(1)} all-to-all(f32[32,896,1]{1,2,0:T(1,128)S(1)} %bitcast.14), channel_id=1, replica_groups=mesh['gx'=8,'gy'=4] {'gx','gy'}, dimensions={0} | all-to-all | bytes 229376 | tf_op jit(solution)/shard_map/all_to_all | solution.py:294
  18.0 2.9 %owner.1 = (f32[64,128]{1,0:T(8,128)S(1)}, f32[4,8]{1,0:T(4,128)}) custom-call(f32[224,128]{1,0:T(8,128)S(1)} %bitcast.12, f32[1,128]{1,0:T(1,128)S(1)} %get-tuple-element.16.limit_ref), custom_call_target="tpu_custom_call" | custom-call | tf_op jit(solution)/shard_map/owner/pallas_call | solution.py:329
  20.9 0.0 copy-start
  20.9 0.0 copy-start.1
  20.9 9.1 %all_to_all.19 = f32[32,256,1]{1,2,0:T(1,128)S(1)} all-to-all(f32[32,256,1]{1,2,0:T(1,128)S(1)} %bitcast.15), channel_id=1, replica_groups=mesh['gx'=8,'gy'=4] {'gx','gy'}, dimensions={0} | all-to-all | bytes 65536 | tf_op jit(solution)/shard_map/all_to_all | solution.py:294
  30.0 0.0 copy-done
  30.0 0.0 copy-done.1
  30.0 1.3 %final.1 = (s32[1,2048]{1,0:T(1,128)}, f32[1,2048]{1,0:T(1,128)}, f32[1,2048]{1,0:T(1,128)}) custom-call(s32[1,2048]{1,0:T(1,128)S(1)} %get-tuple-element.13.code_ref, s32[1,2048]{1,0:T(1,128)S(1)} %bitcast.17, s32[1,256]{1,0:T(1,128)S(1)} %get-tuple-element.14.owner_ref, f32[3,2048]{1,0:T(4,128)S(1)} %copy-done, f32[64,128]{1,0:T(8,128)S(1)} %bitcast.13), custom_call_target="tpu_custom_call" | custom-call | tf_op jit(solution)/shard_map/final/pallas_call | solution.py:339
Async XLA Ops:
  20.9 9.1 %copy-start = (f32[3,2048]{1,0:T(4,128)S(1)}, f32[3,2048]{1,0:T(4,128)}, u32[]{:S(2)}) copy-start(f32[3,2048]{1,0:T(4,128)} %vel_ref.1) | copy-start | bytes 73732
  20.9 9.1 %copy-start.1 = (s32[2048,1]{0,1:T(1,128)S(1)}, s32[2048,1]{0,1:T(1,128)}, u32[]{:S(2)}) copy-start(s32[2048,1]{0,1:T(1,128)} %param.9) | copy-start | bytes 24580

commit v3 on v2

--- a/solution.py
+++ b/solution.py
@@ -10,7 +10,6 @@
 CAP = 2048
 LANES = 128
 CHUNK = 256
-CODE = 64
 FIELDS = 7
 softening_sq = 0.0025
 F32 = jnp.float32
@@ -36,13 +35,13 @@
 
 def send_kernel(
     devices, owned, me_ref, label_hbm, owner_hbm, cap_hbm, pos_hbm, vel_hbm, mass_hbm,
-    out_ref, code_ref, limit_ref, owner_out,
-    label_ref, owner_ref, cap_ref, pos_ref, vel_ref, mass_ref, parts_ref, hit_ref, spread_ref, block_ref, sems,
+    out_ref, rank_ref, limit_ref, hit_ref, order_ref,
+    label_ref, owner_ref, cap_ref, pos_ref, vel_ref, mass_ref, parts_ref, spread_ref, sems,
 ):
     count = label_ref.shape[1]
     groups = devices * owned
     span = LANES // owned
-    shift = owned.bit_length() - 1
+    chunks = count // CHUNK
     copies = [
         pltpu.make_async_copy(source, target, sems.at[k])
         for k, (source, target) in enumerate(
@@ -61,10 +60,50 @@
     rows = iota((groups, 1), 0)
     upto = (iota((CHUNK, CHUNK), 0) <= iota((CHUNK, CHUNK), 1)).astype(F32).astype(BF16)
     copies[0].wait()
-    inverse = inverse_column(owner_ref[...], rows)
-    owner_out[...] = owner_ref[...]
+    inverse = inverse_column(owner_ref[...], (rows % devices) * owned + rows // devices)
     for copy in copies[1:]:
         copy.wait()
+
+    kind = BF16 if groups <= 256 else F32
+    name = jnp.broadcast_to(inverse, (groups, CHUNK)).astype(kind)
+    for chunk in range(chunks):
+        cols = slice(chunk * CHUNK, (chunk + 1) * CHUNK)
+        label = label_ref[:, cols].astype(F32).astype(kind)
+        hit_ref[:, cols] = jnp.where(label == name, jnp.ones((), kind), jnp.zeros((), kind)).astype(BF16)
+    prefixes = [jnp.dot(hit_ref[:, chunk * CHUNK : (chunk + 1) * CHUNK], upto, preferred_element_type=F32) for chunk in range(chunks)]
+
+    fields = jnp.concatenate([pos_ref[...], vel_ref[...], mass_ref[...], jnp.zeros((1, count), F32)], axis=0)
+    for k, part in enumerate(parts_of(fields)):
+        for chunk in range(chunks):
+            parts_ref[chunk * 24 + k * 8 : chunk * 24 + k * 8 + 8, :] = part[:, chunk * CHUNK : (chunk + 1) * CHUNK]
+
+    base = jnp.zeros((groups, CHUNK), BF16)
+    ranks = iota((span, 1), 0)
+    for chunk in range(chunks):
+        cols = slice(chunk * CHUNK, (chunk + 1) * CHUNK)
+        prefix = prefixes[chunk]
+        mine = (prefix.astype(BF16) + base) * hit_ref[:, cols]
+        base = base + jnp.broadcast_to(prefix[:, CHUNK - 1 : CHUNK], (groups, CHUNK)).astype(BF16)
+        while mine.shape[0] > 16:
+            half = mine.shape[0] // 2
+            mine = mine[0:half] + mine[half:]
+        rank = jnp.sum(mine.astype(F32), axis=0, keepdims=True).astype(jnp.int32) - 1
+        rank_ref[:, cols] = rank
+        here = rank == ranks
+        for k in range(3):
+            for f in range(FIELDS):
+                row = parts_ref[pl.ds(chunk * 24 + k * 8 + f, span, stride=0), :]
+                first = (k * FIELDS + f) * span
+                spread_ref[first : first + span, cols] = jnp.where(
+                    here, row, 0.0
+                ).astype(BF16)
+
+    found = lax.dot_general(
+        spread_ref[...], hit_ref[...], (((1,), (1,)), ((), ())), preferred_element_type=F32
+    )
+    size = FIELDS * span
+    found = (found[0:size] + found[size : 2 * size]) + found[2 * size :]
+    found = jnp.concatenate([found, jnp.zeros((LANES - size, groups), F32)], axis=0)
 
     slots = me_ref[0, 0] * owned + iota((owned, 1), 0)
     limit_col = jnp.sum(
@@ -76,41 +115,11 @@
     limit_ref[...] = jnp.sum(
         jnp.where(segment == iota((owned, 1), 0), limit_col, 0.0), axis=0, keepdims=True
     )
-
-    fields = jnp.concatenate([pos_ref[...], vel_ref[...], mass_ref[...], jnp.zeros((1, count), F32)], axis=0)
-    for k, part in enumerate(parts_of(fields)):
-        for chunk in range(count // CHUNK):
-            parts_ref[chunk * 24 + k * 8 : chunk * 24 + k * 8 + 8, :] = part[:, chunk * CHUNK : (chunk + 1) * CHUNK]
-        spread_ref[k * LANES + FIELDS * span : (k + 1) * LANES, :] = jnp.zeros((span, count), BF16)
-
-    base = jnp.broadcast_to((rows * CODE).astype(F32), (groups, LANES))
-    ranks = iota((span, 1), 0)
-    for chunk in range(count // CHUNK):
-        cols = slice(chunk * CHUNK, (chunk + 1) * CHUNK)
-        hit = label_ref[:, cols].astype(F32) == inverse
-        packed = jnp.where(hit, 1.0, 0.0).astype(BF16)
-        hit_ref[:, cols] = packed
-        prefix = jnp.dot(packed, upto, preferred_element_type=F32)
-        wide = jnp.concatenate([base] * (CHUNK // LANES), axis=1)
-        value = jnp.sum(jnp.where(hit, prefix + wide, 0.0), axis=0, keepdims=True)
-        base = base + prefix[:, CHUNK - 1 : CHUNK]
-        code = value.astype(jnp.int32) - 1
-        slot = code >> 6
-        rank = code & (CODE - 1)
-        code_ref[:, cols] = (((slot & (owned - 1)) * devices + (slot >> shift)) << 6) + rank
-        mine = rank == ranks
-        for k in range(3):
-            for f in range(FIELDS):
-                row = parts_ref[pl.ds(chunk * 24 + k * 8 + f, span, stride=0), :]
-                spread_ref[k * LANES + f * span : k * LANES + (f + 1) * span, cols] = jnp.where(
-                    mine, row, 0.0
-                ).astype(BF16)
-
-    found = lax.dot_general(
-        hit_ref[...], spread_ref[...], (((1,), (1,)), ((), ())), preferred_element_type=F32
-    )
-    block_ref[...] = (found[:, 0:LANES] + found[:, LANES : 2 * LANES]) + found[:, 2 * LANES :]
-    block = [block_ref[pl.ds(g, devices, stride=owned), :] for g in range(owned)]
+    inverse_row = jnp.sum(jnp.where(rows == iota((1, groups), 1), inverse, 0.0), axis=0, keepdims=True)
+    order_ref[...] = jnp.where(inverse < inverse_row, 1.0, 0.0).astype(BF16)
+
+    found = jnp.transpose(found)
+    block = [found[g * devices : (g + 1) * devices] for g in range(owned)]
     step = owned // 2
     while step:
         upper = (segment & step) != 0
@@ -125,7 +134,7 @@
         out_ref[pl.ds(f, devices, stride=FIELDS), :] = block[f]
 
 
-def owner_kernel(devices, owned, got_ref, limit_ref, out_ref, stats_ref):
+def owner_kernel(devices, owned, got_ref, limit_ref, out_ref, stats_ref, far_ref):
     span = LANES // owned
     blocks = devices // 8
     lane = iota((1, LANES), 1)
@@ -169,21 +178,25 @@
 
     near = [[x[b * 8 : b * 8 + 8] for b in range(blocks)] for x in (field[0], field[1], field[2], mass)]
 
-    def pair_block(turned, diagonal, one_way, off_diagonal, acc):
+    def pair_block(turned, diagonal, one_way, slot, acc):
         acc = list(acc)
         far_sum = [None] * blocks
+        for k in range(4 * blocks):
+            far_ref[slot, k * 16 : k * 16 + 8, :] = turned[k]
+            far_ref[slot, k * 16 + 8 : k * 16 + 16, :] = turned[k]
         for shift in range(8):
             on_diag = shift in diagonal
             single = shift in one_way
             for b in range(blocks):
-                others = list(range(b)) if off_diagonal else []
+                others = list(range(b))
                 if on_diag or single:
                     others.append(b)
                 if not others:
                     continue
                 far = [turned[k * blocks + b] for k in range(4)]
                 if shift:
-                    far = [pltpu.roll(x, 8 - shift, 0) for x in far]
+                    starts = [(k * blocks + b) * 16 + shift for k in range(4)]
+                    far = [far_ref[slot, start : start + 8, :] for start in starts]
                 back = None
                 for a in others:
                     dx = near[0][a] - far[0]
@@ -207,25 +220,25 @@
     flat = [near[k][b] for k in range(4) for b in range(blocks)]
     zeros = [jnp.zeros((8, LANES), F32)] * blocks
 
-    def turn(diagonal, one_way, _, carry):
+    def turn(diagonal, one_way, step, carry):
         turned, acc, far = carry
         turned = [spin(x) for x in turned]
-        acc, extra = pair_block(turned, diagonal, one_way, True, acc)
+        acc, extra = pair_block(turned, diagonal, one_way, step % 2, acc)
         far = [spin(x + y) for x, y in zip(far, extra)]
         return turned, acc, far
 
     def repeat(diagonal, carry):
         if blocks > 4:
             return lax.fori_loop(1, half, functools.partial(turn, diagonal, ()), carry)
-        for _ in range(1, half):
-            carry = turn(diagonal, (), 0, carry)
+        for step in range(1, half):
+            carry = turn(diagonal, (), step, carry)
         return carry
 
     carry = repeat((), (flat, zeros, zeros))
     carry = turn((1, 2, 3), (0, 4), 0, carry)
     carry = repeat(every, carry)
     _, acc, far = carry
-    acc, extra = pair_block(flat, (1, 2, 3), (4,), True, acc)
+    acc, extra = pair_block(flat, (1, 2, 3), (4,), 0, acc)
     pot = jnp.concatenate([x + (y + z) for x, y, z in zip(acc, far, extra)], axis=0) / -CAP
 
     wide = functools.partial(jnp.broadcast_to, shape=(devices, LANES))
@@ -236,15 +249,12 @@
     out_ref[pl.ds(1, devices, stride=2), :] = more
 
 
-def final_kernel(
-    devices, owned, code_ref, label_ref, owner_ref, vel_ref, got_ref, index_ref, pot_ref, bind_ref
-):
-    count = code_ref.shape[1]
+def final_kernel(devices, owned, rank_ref, hit_ref, order_ref, vel_ref, got_ref, index_ref, pot_ref, bind_ref):
+    count = rank_ref.shape[1]
     groups = devices * owned
     span = LANES // owned
+    used = 2 * span
     lane = iota((1, LANES), 1)
-    rows = iota((groups, 1), 0)
-    inverse = inverse_column(owner_ref[...], (rows % devices) * owned + rows // devices)
     pots = got_ref[pl.ds(0, devices, stride=2), :]
     more = got_ref[pl.ds(1, devices, stride=2), :]
     table = []
@@ -252,21 +262,20 @@
         left = pots if group == 0 else pltpu.roll(pots, LANES - group * span, 1)
         right = pltpu.roll(more, (LANES + span - group * span) % LANES, 1) if group != 1 else more
         table.append(jnp.where(lane < span, left, right))
-    table = jnp.transpose(jnp.concatenate(table, axis=0))[0 : 2 * span]
+    table = jnp.transpose(jnp.concatenate(table, axis=0))[0:used]
     parts = parts_of(table)
-    counted = jnp.concatenate([part[2 * span - 8 :] for part in parts[0:2]], axis=0).astype(BF16)
-    parts = jnp.concatenate(parts, axis=0).astype(BF16)
-    used = 2 * span
+    counted = jnp.concatenate([part[used - 8 :] for part in parts[0:2]], axis=0).astype(BF16)
+    starts = jnp.dot(counted, order_ref[...], preferred_element_type=F32)
+    starts = jnp.broadcast_to(starts[7:8] + starts[15:16], (8, groups))
+    parts = jnp.concatenate([*parts, *parts_of(starts)], axis=0).astype(BF16)
     for chunk in range(count // CHUNK):
         cols = slice(chunk * CHUNK, (chunk + 1) * CHUNK)
-        code = code_ref[:, cols]
-        rank = code & (CODE - 1)
-        hit = jnp.where(code >> 6 == rows, 1.0, 0.0).astype(BF16)
-        lower = jnp.where(inverse < label_ref[:, cols].astype(F32), 1.0, 0.0).astype(BF16)
-        found = jnp.dot(parts, hit, preferred_element_type=F32)
-        found = (found[0:used] + found[used : 2 * used]) + found[2 * used :]
-        starts = jnp.dot(counted, lower, preferred_element_type=F32)
-        start = starts[7:8] + starts[15:16]
+        rank = rank_ref[:, cols]
+        found = jnp.dot(parts, hit_ref[:, cols], preferred_element_type=F32)
+        start = (found[3 * used : 3 * used + 1] + found[3 * used + 8 : 3 * used + 9]) + found[
+            3 * used + 16 : 3 * used + 17
+        ]
+        found = (found[0:used] + found[used : 2 * used]) + found[2 * used : 3 * used]
         pot = jnp.sum(jnp.where(iota((span, 1), 0) == rank, found[0:span], 0.0), axis=0, keepdims=True)
         prefix = found[span + 3 : span + 4]
         kept = found[used - 1 : used]
@@ -294,13 +303,14 @@
         flat = lax.all_to_all(flat, ("gx", "gy"), split_axis=0, concat_axis=0, tiled=True)
         return flat.reshape(devices * rows, LANES)
 
-    outgoing, code, limit, owner_kept = pl.pallas_call(
+    outgoing, rank, limit, hit, order = pl.pallas_call(
         functools.partial(send_kernel, devices, owned),
         out_shape=(
             jax.ShapeDtypeStruct((devices * FIELDS, LANES), F32),
             jax.ShapeDtypeStruct((1, count), jnp.int32),
             jax.ShapeDtypeStruct((1, LANES), F32),
-            jax.ShapeDtypeStruct((1, groups), jnp.int32),
+            jax.ShapeDtypeStruct((groups, count), BF16),
+            jax.ShapeDtypeStruct((groups, groups), BF16),
         ),
         in_specs=[pl.BlockSpec(memory_space=pltpu.SMEM)] + [pl.BlockSpec(memory_space=pltpu.HBM)] * 6,
         scratch_shapes=[
@@ -311,9 +321,7 @@
             pltpu.VMEM((3, count), F32),
             pltpu.VMEM((1, count), F32),
             pltpu.VMEM((24 * count // CHUNK, CHUNK), F32),
-            pltpu.VMEM((groups, count), BF16),
-            pltpu.VMEM((3 * LANES, count), BF16),
-            pltpu.VMEM((groups, LANES), F32),
+            pltpu.VMEM((3 * FIELDS * LANES // owned, count), BF16),
             pltpu.SemaphoreType.DMA((6,)),
         ],
         compiler_params=params,
@@ -332,6 +340,7 @@
             jax.ShapeDtypeStruct((devices * 2, LANES), F32),
             jax.ShapeDtypeStruct((4, owned), F32),
         ),
+        scratch_shapes=[pltpu.VMEM((2, devices * 8, LANES), F32)],
         compiler_params=params,
         name="owner",
     )(received, limit)
@@ -345,7 +354,7 @@
         ),
         compiler_params=params,
         name="final",
-    )(code, label_row, owner_kept, velocities, returned)
+    )(rank, hit, order, velocities, returned)
     return index.reshape(count), potential.reshape(count), binding.reshape(count), catalog
 
 

time: 31.5 us -> 31.3 us (level)
  no operation moved by 1% of the time
where the time goes in v3:
time: 31.3 us; the launch traced here: 31 us
  blocking collectives  24.2 us (77%)
  Pallas kernels  6.17 us (20%)
  between operations  0.65 us (2%)
    all_to_all x2, blocking collectives, exchange(): lax.all_to_all(flat, ('gx', 'gy'), split_axis=0, concat_axis=0, tiled=True)  24.2 us
    pallas_call x1, Pallas kernels, shards(): pl.pallas_call(functools.partial(owner_kernel, devices, owned), out_shape...  2.8 us
    pallas_call x1, Pallas kernels, shards(): pl.pallas_call(functools.partial(send_kernel, devices, owned), out_shape=...  2.2 us
    pallas_call x1, Pallas kernels, shards(): pl.pallas_call(functools.partial(final_kernel, devices, owned), out_shape...  1.17 us

profile of v3, /device:TPU:0, one launch (start us, length us, event | category | flops | bytes accessed | tf_op | source)
XLA Modules:
  0.0 31.0 jit_solution(9647987424810209226)
XLA Ops:
  0.6 2.2 %send.1 = (f32[224,128]{1,0:T(8,128)S(1)}, s32[1,2048]{1,0:T(1,128)S(1)}, f32[1,128]{1,0:T(1,128)S(1)}, bf16[256,2048]{1,0:T(8,128)(2,1)S(1)}, bf16[256,256]{1,0:T(8,128)(2,1)S(1)}) custom-call(s32[1,1]{1,0:T(1,128)} %bitcast.me_ref, s32[1,2048]{1,0:T(1,128)} %bitcast.16, s32[1,256]{1,0:T(1,128)} %bitcast.18, s32[1,256]{1,0:T(1,128)} %bitcast.19, ...), custom_call_target="tpu_custom_call" | custom-call | tf_op jit(solution)/shard_map/send/pallas_call | solution.py:306
  2.8 15.1 %all_to_all.18 = f32[32,896,1]{1,2,0:T(1,128)S(1)} all-to-all(f32[32,896,1]{1,2,0:T(1,128)S(1)} %bitcast.14), channel_id=1, replica_groups=mesh['gx'=8,'gy'=4] {'gx','gy'}, dimensions={0} | all-to-all | bytes 229376 | tf_op jit(solution)/shard_map/all_to_all | solution.py:303
  18.0 2.8 %owner.1 = (f32[64,128]{1,0:T(8,128)S(1)}, f32[4,8]{1,0:T(4,128)}) custom-call(f32[224,128]{1,0:T(8,128)S(1)} %bitcast.12, f32[1,128]{1,0:T(1,128)S(1)} %get-tuple-element.18.limit_ref), custom_call_target="tpu_custom_call" | custom-call | tf_op jit(solution)/shard_map/owner/pallas_call | solution.py:337
  20.8 0.0 copy-start
  20.8 9.1 %all_to_all.19 = f32[32,256,1]{1,2,0:T(1,128)S(1)} all-to-all(f32[32,256,1]{1,2,0:T(1,128)S(1)} %bitcast.15), channel_id=1, replica_groups=mesh['gx'=8,'gy'=4] {'gx','gy'}, dimensions={0} | all-to-all | bytes 65536 | tf_op jit(solution)/shard_map/all_to_all | solution.py:303
  29.8 0.0 copy-done
  29.8 1.2 %final.1 = (s32[1,2048]{1,0:T(1,128)}, f32[1,2048]{1,0:T(1,128)}, f32[1,2048]{1,0:T(1,128)}) custom-call(s32[1,2048]{1,0:T(1,128)S(1)} %get-tuple-element.14.rank_ref, bf16[256,2048]{1,0:T(8,128)(2,1)S(1)} %get-tuple-element.15.hit_ref, bf16[256,256]{1,0:T(8,128)(2,1)S(1)} %get-tuple-element.16.order_ref, f32[3,2048]{1,0:T(4,128)S(1)} %copy-done, ...), custom_call_target="tpu_custom_call" | custom-call | tf_op jit(solution)/shard_map/final/pallas_call | solution.py:348
Async XLA Ops:
  20.8 9.1 %copy-start = (f32[3,2048]{1,0:T(4,128)S(1)}, f32[3,2048]{1,0:T(4,128)}, u32[]{:S(2)}) copy-start(f32[3,2048]{1,0:T(4,128)} %vel_ref.1) | copy-start | bytes 73732

commit v4 on v3

--- a/solution.py
+++ b/solution.py
@@ -35,8 +35,8 @@
 
 def send_kernel(
     devices, owned, me_ref, label_hbm, owner_hbm, cap_hbm, pos_hbm, vel_hbm, mass_hbm,
-    out_ref, rank_ref, limit_ref, hit_ref, order_ref,
-    label_ref, owner_ref, cap_ref, pos_ref, vel_ref, mass_ref, parts_ref, spread_ref, sems,
+    out_ref, rank_ref, limit_ref, hit_out, order_ref,
+    label_ref, owner_ref, cap_ref, pos_ref, vel_ref, mass_ref, parts_ref, hit_ref, spread_ref, sems,
 ):
     count = label_ref.shape[1]
     groups = devices * owned
@@ -68,8 +68,12 @@
     name = jnp.broadcast_to(inverse, (groups, CHUNK)).astype(kind)
     for chunk in range(chunks):
         cols = slice(chunk * CHUNK, (chunk + 1) * CHUNK)
-        label = label_ref[:, cols].astype(F32).astype(kind)
-        hit_ref[:, cols] = jnp.where(label == name, jnp.ones((), kind), jnp.zeros((), kind)).astype(BF16)
+        label = jnp.broadcast_to(label_ref[:, cols].astype(F32), (16, CHUNK)).astype(kind)
+        for row in range(0, groups, 16):
+            here = slice(row, row + 16)
+            hit = jnp.where(label == name[here], jnp.ones((), kind), jnp.zeros((), kind)).astype(BF16)
+            hit_ref[here, cols] = hit
+            hit_out[here, cols] = hit
     prefixes = [jnp.dot(hit_ref[:, chunk * CHUNK : (chunk + 1) * CHUNK], upto, preferred_element_type=F32) for chunk in range(chunks)]
 
     fields = jnp.concatenate([pos_ref[...], vel_ref[...], mass_ref[...], jnp.zeros((1, count), F32)], axis=0)
@@ -78,7 +82,7 @@
             parts_ref[chunk * 24 + k * 8 : chunk * 24 + k * 8 + 8, :] = part[:, chunk * CHUNK : (chunk + 1) * CHUNK]
 
     base = jnp.zeros((groups, CHUNK), BF16)
-    ranks = iota((span, 1), 0)
+    ranks = iota((span, 1), 0).astype(F32)
     for chunk in range(chunks):
         cols = slice(chunk * CHUNK, (chunk + 1) * CHUNK)
         prefix = prefixes[chunk]
@@ -87,8 +91,8 @@
         while mine.shape[0] > 16:
             half = mine.shape[0] // 2
             mine = mine[0:half] + mine[half:]
-        rank = jnp.sum(mine.astype(F32), axis=0, keepdims=True).astype(jnp.int32) - 1
-        rank_ref[:, cols] = rank
+        rank = jnp.sum(mine.astype(F32), axis=0, keepdims=True) - 1.0
+        rank_ref[:, cols] = rank.astype(jnp.int32)
         here = rank == ranks
         for k in range(3):
             for f in range(FIELDS):
@@ -103,8 +107,6 @@
     )
     size = FIELDS * span
     found = (found[0:size] + found[size : 2 * size]) + found[2 * size :]
-    found = jnp.concatenate([found, jnp.zeros((LANES - size, groups), F32)], axis=0)
-
     slots = me_ref[0, 0] * owned + iota((owned, 1), 0)
     limit_col = jnp.sum(
         jnp.where(owner_ref[...] == slots, jnp.minimum(cap_ref[...], CAP).astype(F32), 0.0),
@@ -118,20 +120,31 @@
     inverse_row = jnp.sum(jnp.where(rows == iota((1, groups), 1), inverse, 0.0), axis=0, keepdims=True)
     order_ref[...] = jnp.where(inverse < inverse_row, 1.0, 0.0).astype(BF16)
 
-    found = jnp.transpose(found)
-    block = [found[g * devices : (g + 1) * devices] for g in range(owned)]
-    step = owned // 2
-    while step:
-        upper = (segment & step) != 0
-        for low in range(owned):
-            if low & step:
-                continue
-            one, two = block[low], block[low + step]
-            block[low] = jnp.where(upper, pltpu.roll(two, step * span, 1), one)
-            block[low + step] = jnp.where(upper, two, pltpu.roll(one, LANES - step * span, 1))
-        step //= 2
-    for f in range(FIELDS):
-        out_ref[pl.ds(f, devices, stride=FIELDS), :] = block[f]
+    block = max(1, LANES // devices)
+    upper = iota((1, LANES), 1) // devices
+    tiles = []
+    for tile in range(owned // block):
+        lanes = slice(tile * LANES, (tile + 1) * LANES)
+        piece = [found[f * span : (f + 1) * span, lanes] for f in range(FIELDS)]
+        piece += [jnp.zeros((span, LANES), F32)] * (-FIELDS % block)
+        step = block // 2
+        while step:
+            far = (upper & step) != 0
+            for low in range(len(piece)):
+                if low & step:
+                    continue
+                one, two = piece[low], piece[low + step]
+                piece[low] = jnp.where(far, pltpu.roll(two, step * devices, 1), one)
+                piece[low + step] = jnp.where(far, two, pltpu.roll(one, LANES - step * devices, 1))
+            step //= 2
+        tiles.append(piece)
+    for first in range(0, FIELDS, block):
+        turned = jnp.transpose(
+            jnp.concatenate([piece[first + k] for piece in tiles for k in range(block)], axis=0)
+        )
+        for f in range(first, min(first + block, FIELDS)):
+            low = (f - first) * devices
+            out_ref[pl.ds(f, devices, stride=FIELDS), :] = turned[low : low + devices]
 
 
 def owner_kernel(devices, owned, got_ref, limit_ref, out_ref, stats_ref, far_ref):
@@ -254,15 +267,25 @@
     groups = devices * owned
     span = LANES // owned
     used = 2 * span
-    lane = iota((1, LANES), 1)
-    pots = got_ref[pl.ds(0, devices, stride=2), :]
-    more = got_ref[pl.ds(1, devices, stride=2), :]
+    block = max(1, LANES // devices)
+    both = [got_ref[pl.ds(k, devices, stride=2), :] for k in range(2)]
+    both += [jnp.zeros((-2 * devices % LANES, LANES), F32)] if 2 * devices % LANES else []
+    turned = jnp.transpose(jnp.concatenate(both, axis=0))
+    place = iota((1, LANES), 1) // devices
     table = []
-    for group in range(owned):
-        left = pots if group == 0 else pltpu.roll(pots, LANES - group * span, 1)
-        right = pltpu.roll(more, (LANES + span - group * span) % LANES, 1) if group != 1 else more
-        table.append(jnp.where(lane < span, left, right))
-    table = jnp.transpose(jnp.concatenate(table, axis=0))[0:used]
+    for k in range(2):
+        tile, offset = divmod(k * devices, LANES)
+        row = []
+        for first in range(0, owned, block):
+            filled = None
+            for j in range(block):
+                piece = turned[(first + j) * span : (first + j + 1) * span, tile * LANES : (tile + 1) * LANES]
+                shift = (j * devices - offset) % LANES
+                piece = pltpu.roll(piece, shift, 1) if shift else piece
+                filled = piece if filled is None else jnp.where(place == j, piece, filled)
+            row.append(filled)
+        table.append(jnp.concatenate(row, axis=1))
+    table = jnp.concatenate(table, axis=0)
     parts = parts_of(table)
     counted = jnp.concatenate([part[used - 8 :] for part in parts[0:2]], axis=0).astype(BF16)
     starts = jnp.dot(counted, order_ref[...], preferred_element_type=F32)
@@ -321,6 +344,7 @@
             pltpu.VMEM((3, count), F32),
             pltpu.VMEM((1, count), F32),
             pltpu.VMEM((24 * count // CHUNK, CHUNK), F32),
+            pltpu.VMEM((groups, count), BF16),
             pltpu.VMEM((3 * FIELDS * LANES // owned, count), BF16),
             pltpu.SemaphoreType.DMA((6,)),
         ],

time: 31.3 us -> 31.1 us (level)
  no operation moved by 1% of the time
where the time goes in v4:
time: 31.1 us; the launch traced here: 30.9 us
  blocking collectives  24.2 us (78%)
  Pallas kernels  6.02 us (19%)
  between operations  0.65 us (2%)
    all_to_all x2, blocking collectives, exchange(): lax.all_to_all(flat, ('gx', 'gy'), split_axis=0, concat_axis=0, tiled=True)  24.2 us
    pallas_call x1, Pallas kernels, shards(): pl.pallas_call(functools.partial(owner_kernel, devices, owned), out_shape...  2.8 us
    pallas_call x1, Pallas kernels, shards(): pl.pallas_call(functools.partial(send_kernel, devices, owned), out_shape=...  2.03 us
    pallas_call x1, Pallas kernels, shards(): pl.pallas_call(functools.partial(final_kernel, devices, owned), out_shape...  1.18 us

profile of v4, /device:TPU:0, one launch (start us, length us, event | category | flops | bytes accessed | tf_op | source)
XLA Modules:
  0.0 30.9 jit_solution(6999311621064669501)
XLA Ops:
  0.6 2.0 %send.1 = (f32[224,128]{1,0:T(8,128)S(1)}, s32[1,2048]{1,0:T(1,128)S(1)}, f32[1,128]{1,0:T(1,128)S(1)}, bf16[256,2048]{1,0:T(8,128)(2,1)S(1)}, bf16[256,256]{1,0:T(8,128)(2,1)S(1)}) custom-call(s32[1,1]{1,0:T(1,128)} %bitcast.me_ref, s32[1,2048]{1,0:T(1,128)} %bitcast.16, s32[1,256]{1,0:T(1,128)} %bitcast.18, s32[1,256]{1,0:T(1,128)} %bitcast.19, ...), custom_call_target="tpu_custom_call" | custom-call | tf_op jit(solution)/shard_map/send/pallas_call | solution.py:329
  2.7 15.1 %all_to_all.18 = f32[32,896,1]{1,2,0:T(1,128)S(1)} all-to-all(f32[32,896,1]{1,2,0:T(1,128)S(1)} %bitcast.14), channel_id=1, replica_groups=mesh['gx'=8,'gy'=4] {'gx','gy'}, dimensions={0} | all-to-all | bytes 229376 | tf_op jit(solution)/shard_map/all_to_all | solution.py:326
  17.8 2.8 %owner.1 = (f32[64,128]{1,0:T(8,128)S(1)}, f32[4,8]{1,0:T(4,128)}) custom-call(f32[224,128]{1,0:T(8,128)S(1)} %bitcast.12, f32[1,128]{1,0:T(1,128)S(1)} %get-tuple-element.18.limit_ref), custom_call_target="tpu_custom_call" | custom-call | tf_op jit(solution)/shard_map/owner/pallas_call | solution.py:361
  20.6 0.0 copy-start
  20.6 9.1 %all_to_all.19 = f32[32,256,1]{1,2,0:T(1,128)S(1)} all-to-all(f32[32,256,1]{1,2,0:T(1,128)S(1)} %bitcast.15), channel_id=1, replica_groups=mesh['gx'=8,'gy'=4] {'gx','gy'}, dimensions={0} | all-to-all | bytes 65536 | tf_op jit(solution)/shard_map/all_to_all | solution.py:326
  29.7 0.0 copy-done
  29.7 1.2 %final.1 = (s32[1,2048]{1,0:T(1,128)}, f32[1,2048]{1,0:T(1,128)}, f32[1,2048]{1,0:T(1,128)}) custom-call(s32[1,2048]{1,0:T(1,128)S(1)} %get-tuple-element.14.rank_ref, bf16[256,2048]{1,0:T(8,128)(2,1)S(1)} %get-tuple-element.15.hit_ref, bf16[256,256]{1,0:T(8,128)(2,1)S(1)} %get-tuple-element.16.order_ref, f32[3,2048]{1,0:T(4,128)S(1)} %copy-done, ...), custom_call_target="tpu_custom_call" | custom-call | tf_op jit(solution)/shard_map/final/pallas_call | solution.py:372
Async XLA Ops:
  20.6 9.1 %copy-start = (f32[3,2048]{1,0:T(4,128)S(1)}, f32[3,2048]{1,0:T(4,128)}, u32[]{:S(2)}) copy-start(f32[3,2048]{1,0:T(4,128)} %vel_ref.1) | copy-start | bytes 73732

commit v5 on v4

--- a/solution.py
+++ b/solution.py
@@ -92,7 +92,9 @@
             half = mine.shape[0] // 2
             mine = mine[0:half] + mine[half:]
         rank = jnp.sum(mine.astype(F32), axis=0, keepdims=True) - 1.0
-        rank_ref[:, cols] = rank.astype(jnp.int32)
+        for part in range(CHUNK // LANES):
+            line = chunk * (CHUNK // LANES) + part
+            rank_ref[line : line + 1, :] = rank[:, part * LANES : (part + 1) * LANES]
         here = rank == ranks
         for k in range(3):
             for f in range(FIELDS):
@@ -262,8 +264,8 @@
     out_ref[pl.ds(1, devices, stride=2), :] = more
 
 
-def final_kernel(devices, owned, rank_ref, hit_ref, order_ref, vel_ref, got_ref, index_ref, pot_ref, bind_ref):
-    count = rank_ref.shape[1]
+def final_kernel(devices, owned, rank_ref, hit_ref, order_ref, vel_ref, got_ref, index_ref, pot_ref, bind_ref, dense_ref):
+    count = vel_ref.shape[1]
     groups = devices * owned
     span = LANES // owned
     used = 2 * span
@@ -291,23 +293,32 @@
     starts = jnp.dot(counted, order_ref[...], preferred_element_type=F32)
     starts = jnp.broadcast_to(starts[7:8] + starts[15:16], (8, groups))
     parts = jnp.concatenate([*parts, *parts_of(starts)], axis=0).astype(BF16)
+    lines = CHUNK // LANES
     for chunk in range(count // CHUNK):
         cols = slice(chunk * CHUNK, (chunk + 1) * CHUNK)
-        rank = rank_ref[:, cols]
+        rank = jnp.concatenate(
+            [rank_ref[line : line + 1, :] for line in range(chunk * lines, (chunk + 1) * lines)], axis=1
+        )
         found = jnp.dot(parts, hit_ref[:, cols], preferred_element_type=F32)
         start = (found[3 * used : 3 * used + 1] + found[3 * used + 8 : 3 * used + 9]) + found[
             3 * used + 16 : 3 * used + 17
         ]
         found = (found[0:used] + found[used : 2 * used]) + found[2 * used : 3 * used]
-        pot = jnp.sum(jnp.where(iota((span, 1), 0) == rank, found[0:span], 0.0), axis=0, keepdims=True)
-        prefix = found[span + 3 : span + 4]
-        kept = found[used - 1 : used]
-        global_rank = prefix + rank.astype(F32)
-        keep = global_rank < kept
+        pot = jnp.sum(
+            jnp.where(iota((span, 1), 0).astype(F32) == rank, found[0:span], 0.0), axis=0, keepdims=True
+        )
         speed = jnp.sum((vel_ref[:, cols] - found[span : span + 3]) ** 2, axis=0, keepdims=True)
-        index_ref[:, cols] = jnp.where(keep, (start + global_rank).astype(jnp.int32), -1)
-        pot_ref[:, cols] = jnp.where(keep, pot, 0.0)
-        bind_ref[:, cols] = jnp.where(keep, 0.5 * speed + pot, 0.0)
+        values = (pot, speed, found[span + 3 : span + 4], found[used - 1 : used], start)
+        for k, value in enumerate(values):
+            for part in range(lines):
+                line = chunk * lines + part
+                dense_ref[k, line : line + 1, :] = value[:, part * LANES : (part + 1) * LANES]
+    pot, speed, prefix, kept, start = [dense_ref[k] for k in range(5)]
+    global_rank = prefix + rank_ref[...]
+    keep = global_rank < kept
+    index_ref[...] = jnp.where(keep, (start + global_rank).astype(jnp.int32), -1)
+    pot_ref[...] = jnp.where(keep, pot, 0.0)
+    bind_ref[...] = jnp.where(keep, 0.5 * speed + pot, 0.0)
 
 
 def shards(positions, velocities, masses, labels, owner_slot, group_cap):
@@ -330,7 +341,7 @@
         functools.partial(send_kernel, devices, owned),
         out_shape=(
             jax.ShapeDtypeStruct((devices * FIELDS, LANES), F32),
-            jax.ShapeDtypeStruct((1, count), jnp.int32),
+            jax.ShapeDtypeStruct((count // LANES, LANES), F32),
             jax.ShapeDtypeStruct((1, LANES), F32),
             jax.ShapeDtypeStruct((groups, count), BF16),
             jax.ShapeDtypeStruct((groups, groups), BF16),
@@ -372,10 +383,11 @@
     index, potential, binding = pl.pallas_call(
         functools.partial(final_kernel, devices, owned),
         out_shape=(
-            jax.ShapeDtypeStruct((1, count), jnp.int32),
-            jax.ShapeDtypeStruct((1, count), F32),
-            jax.ShapeDtypeStruct((1, count), F32),
+            jax.ShapeDtypeStruct((count // LANES, LANES), jnp.int32),
+            jax.ShapeDtypeStruct((count // LANES, LANES), F32),
+            jax.ShapeDtypeStruct((count // LANES, LANES), F32),
         ),
+        scratch_shapes=[pltpu.VMEM((5, count // LANES, LANES), F32)],
         compiler_params=params,
         name="final",
     )(rank, hit, order, velocities, returned)

time: 31.1 us -> 31.1 us (level)
  no operation moved by 1% of the time
where the time goes in v5:
time: 31.1 us; the launch traced here: 30.8 us
  blocking collectives  24.2 us (78%)
  Pallas kernels  6 us (19%)
  between operations  0.65 us (2%)
    all_to_all x2, blocking collectives, exchange(): lax.all_to_all(flat, ('gx', 'gy'), split_axis=0, concat_axis=0, tiled=True)  24.2 us
    pallas_call x1, Pallas kernels, shards(): pl.pallas_call(functools.partial(owner_kernel, devices, owned), out_shape...  2.8 us
    pallas_call x1, Pallas kernels, shards(): pl.pallas_call(functools.partial(send_kernel, devices, owned), out_shape=...  2.02 us
    pallas_call x1, Pallas kernels, shards(): pl.pallas_call(functools.partial(final_kernel, devices, owned), out_shape...  1.18 us

profile of v5, /device:TPU:0, one launch (start us, length us, event | category | flops | bytes accessed | tf_op | source)
XLA Modules:
  0.0 30.8 jit_solution(4998192634215230074)
XLA Ops:
  0.6 2.0 %send.1 = (f32[224,128]{1,0:T(8,128)S(1)}, f32[16,128]{1,0:T(8,128)S(1)}, f32[1,128]{1,0:T(1,128)S(1)}, bf16[256,2048]{1,0:T(8,128)(2,1)S(1)}, bf16[256,256]{1,0:T(8,128)(2,1)S(1)}) custom-call(s32[1,1]{1,0:T(1,128)} %bitcast.me_ref, s32[1,2048]{1,0:T(1,128)} %bitcast.16, s32[1,256]{1,0:T(1,128)} %bitcast.18, s32[1,256]{1,0:T(1,128)} %bitcast.19, ...), custom_call_target="tpu_custom_call" | custom-call | tf_op jit(solution)/shard_map/send/pallas_call | solution.py:340
  2.7 15.1 %all_to_all.18 = f32[32,896,1]{1,2,0:T(1,128)S(1)} all-to-all(f32[32,896,1]{1,2,0:T(1,128)S(1)} %bitcast.14), channel_id=1, replica_groups=mesh['gx'=8,'gy'=4] {'gx','gy'}, dimensions={0} | all-to-all | bytes 229376 | tf_op jit(solution)/shard_map/all_to_all | solution.py:337
  17.8 2.8 %owner.1 = (f32[64,128]{1,0:T(8,128)S(1)}, f32[4,8]{1,0:T(4,128)}) custom-call(f32[224,128]{1,0:T(8,128)S(1)} %bitcast.12, f32[1,128]{1,0:T(1,128)S(1)} %get-tuple-element.18.limit_ref), custom_call_target="tpu_custom_call" | custom-call | tf_op jit(solution)/shard_map/owner/pallas_call | solution.py:372
  20.6 0.0 copy-start
  20.6 9.1 %all_to_all.19 = f32[32,256,1]{1,2,0:T(1,128)S(1)} all-to-all(f32[32,256,1]{1,2,0:T(1,128)S(1)} %bitcast.15), channel_id=1, replica_groups=mesh['gx'=8,'gy'=4] {'gx','gy'}, dimensions={0} | all-to-all | bytes 65536 | tf_op jit(solution)/shard_map/all_to_all | solution.py:337
  29.7 0.0 copy-done
  29.7 1.2 %final.1 = (s32[16,128]{1,0:T(8,128)}, f32[16,128]{1,0:T(8,128)}, f32[16,128]{1,0:T(8,128)}) custom-call(f32[16,128]{1,0:T(8,128)S(1)} %get-tuple-element.14.rank_ref, bf16[256,2048]{1,0:T(8,128)(2,1)S(1)} %get-tuple-element.15.hit_ref, bf16[256,256]{1,0:T(8,128)(2,1)S(1)} %get-tuple-element.16.order_ref, f32[3,2048]{1,0:T(4,128)S(1)} %copy-done, ...), custom_call_target="tpu_custom_call" | custom-call | tf_op jit(solution)/shard_map/final/pallas_call | solution.py:383
Async XLA Ops:
  20.6 9.1 %copy-start = (f32[3,2048]{1,0:T(4,128)S(1)}, f32[3,2048]{1,0:T(4,128)}, u32[]{:S(2)}) copy-start(f32[3,2048]{1,0:T(4,128)} %vel_ref.1) | copy-start | bytes 73732
